TPU v7x, 256 devices: a whole 4x4x8 slice. The times are simulated.
256 devices in a mesh: req: 32 (over x, y, core), tp: 8 (over z).
Axes of the slice: x: 4, y: 4, z: 8, core: 2. Of those that a mesh axis runs over, the one named last changes fastest.
Arguments:
- activations: bfloat16 [4096, 2560], P('req', 'tp'), may hold values from -12 to 12
- norm_gain: float32 [2560], replicated, may hold values from 0.1 to 1.9
- input_proj: bfloat16 [2560, 8, 480], P(None, 'tp'), may hold values from -0.125 to 0.125
- output_proj: bfloat16 [2560, 2560], P('tp'), may hold values from -0.125 to 0.125
- cache_pool: bfloat16 [3008, 8, 20480], P('req', 'tp'), may hold values from -103 to 103
- page_table: int32 [64, 32], replicated, may hold values from 0 to 93, as said below
- rebalance_plan: int32 [64, 32], replicated, may hold values from 0 to 31, as said below
- cached_lengths: int32 [64], replicated, may hold values from 1 to 4096, as said below
- token_positions: int32 [64, 64], replicated, may hold values from 1 to 4159, as said below
Outputs:
- attention_out: float32 [4096, 2560], P('req', 'tp')
Inputs may be any that keep to these rules, and one draw needn't show every extreme that they name: token_positions[r, t] = cached_lengths[r] + t. `cached_lengths`: cached tokens of request r before its new ones; in every draw all requests of some group have 4096. rebalance_plan[r, j] is the request's own group for j < 16 and another group for later pages; page 16 of the first request of group q lies in group (q + 16) % 32; at most 2 of the pages j >= 16 of one group's requests lie in any one other group, and some group receives 2 from one other group in every draw. `page_table`: slot of page j of request r in the pool of group rebalance_plan[r, j]; no two entries of the table name the same group and slot.
All inputs are finite; a program needn't handle non-finite values.
Results may differ from a plain program's by a relative error of at most 0.0095.
The roundings to bfloat16 on the way count: a program that leaves them out, or rounds other values in their place, can miss the bound.
Values may be sent and summed in bfloat16 or wider, within the bound.
A program may use at most 128 MiB of HBM per device.

v0:
```python
import jax
import jax.numpy as jnp
from jax import lax
from jax.sharding import PartitionSpec as P

HD = 80
WINDOW = 4096
PAGE = 128
KEEP = 16
NEW = 64
TAIL = 16


EPSILON = 1e-05
THETA = 10000.0
MASKED = -1e30


def rotate(values, places):
    half_dim = values.shape[-1] // 2
    frequency = THETA ** (-(jnp.arange(half_dim, dtype=jnp.float32) * 2.0 / values.shape[-1]))
    angles = places.astype(jnp.float32)[..., None] * frequency
    cosine = jnp.cos(angles)
    sine_part = jnp.sin(angles)
    front_half = values[..., :half_dim]
    back_half = values[..., half_dim:]
    return jnp.concatenate(
        [front_half * cosine - back_half * sine_part, back_half * cosine + front_half * sine_part],
        axis=-1,
    )


def page_valid(places, lengths_here, page_ids):
    key_pos = page_ids[:, :, None] * PAGE + jnp.arange(PAGE, dtype=jnp.int32)[None, None, :]
    inside = key_pos < lengths_here[:, None, None]
    in_window = places[:, None, :, None] - key_pos[:, :, None, :] < WINDOW
    return inside[:, :, None, :] & in_window


def page_stats(queries, pages, valid):
    head_dim = queries.shape[-1]
    unpacked = pages.reshape(pages.shape[:3] + (-1, 2, head_dim))
    cache_keys = unpacked[..., 0, :]
    cache_values = unpacked[..., 1, :]
    scores = jnp.einsum(
        "rtkgd,rjkpd->rjkgtp", queries, cache_keys, preferred_element_type=jnp.float32
    ) * head_dim ** (-0.5)
    valid_mask = valid[:, :, None, None]
    block_peaks = jnp.max(jnp.where(valid_mask, scores, MASKED), axis=-1)
    probabilities = jnp.where(valid_mask, jnp.exp(scores - block_peaks[..., None]), 0.0).astype(
        jnp.bfloat16
    )
    totals = jnp.sum(probabilities, axis=-1, dtype=jnp.float32)
    value_sums = jnp.einsum(
        "rjkgtp,rjkpd->rjkgtd", probabilities, cache_values, preferred_element_type=jnp.float32
    )
    return (block_peaks, totals, value_sums)


def new_stats(queries, new_keys, new_values):
    head_dim = queries.shape[-1]
    count = queries.shape[1]
    scores = jnp.einsum(
        "rtkgd,rukd->rkgtu", queries, new_keys, preferred_element_type=jnp.float32
    ) * head_dim ** (-0.5)
    causal = jnp.arange(count)[:, None] >= jnp.arange(count)[None, :]
    block_peaks = jnp.max(jnp.where(causal, scores, MASKED), axis=-1)
    probabilities = jnp.where(causal, jnp.exp(scores - block_peaks[..., None]), 0.0).astype(
        jnp.bfloat16
    )
    totals = jnp.sum(probabilities, axis=-1, dtype=jnp.float32)
    value_sums = jnp.einsum(
        "rkgtu,rukd->rkgtd", probabilities, new_values, preferred_element_type=jnp.float32
    )
    return (block_peaks, totals, value_sums)


def fold_blocks(block_peaks, totals, value_sums):
    top_peak = jnp.max(block_peaks, axis=1)
    weights = jnp.exp(block_peaks - top_peak[:, None])
    return (
        top_peak,
        jnp.sum(weights * totals, axis=1),
        jnp.sum(weights[..., None] * value_sums, axis=1),
    )


def join_pair(first_stats, second_stats):
    top_peak = jnp.maximum(first_stats[0], second_stats[0])
    weight_one = jnp.exp(first_stats[0] - top_peak)
    weight_two = jnp.exp(second_stats[0] - top_peak)
    totals = weight_one * first_stats[1] + weight_two * second_stats[1]
    value_sums = weight_one[..., None] * first_stats[2] + weight_two[..., None] * second_stats[2]
    return (top_peak, totals, value_sums)


def local(
    activations,
    norm_gain,
    input_proj,
    output_proj,
    cache_pool,
    page_table,
    rebalance_plan,
    cached_lengths,
    token_positions,
):
    group_index = lax.axis_index("req")
    group_count = lax.axis_size("req")
    tok_rows = activations.shape[0]
    req_here = tok_rows // NEW
    kv_local = input_proj.shape[1]
    model_width = input_proj.shape[0]
    group_size = input_proj.shape[2] // HD - 2
    gathered = lax.all_gather(activations, "tp", axis=1, tiled=True)
    widened = gathered.astype(jnp.float32)
    mean_square = jnp.mean(widened * widened, axis=1, keepdims=True)
    normed = (widened * lax.rsqrt(mean_square + EPSILON) * norm_gain).astype(jnp.bfloat16)
    projected = jnp.dot(
        normed, input_proj.reshape(model_width, -1), preferred_element_type=jnp.float32
    )
    projected = projected.reshape(tok_rows, kv_local, group_size + 2, HD)
    first_row = group_index * req_here
    my_places = lax.dynamic_slice_in_dim(token_positions, first_row, req_here, 0)
    my_lengths = lax.dynamic_slice_in_dim(cached_lengths, first_row, req_here, 0)
    my_table = lax.dynamic_slice_in_dim(page_table, first_row, req_here, 0)
    my_plan = lax.dynamic_slice_in_dim(rebalance_plan, first_row, req_here, 0)
    flat_places = my_places.reshape(tok_rows)
    queries = rotate(
        projected[:, :, :group_size],
        jnp.broadcast_to(flat_places[:, None, None], (tok_rows, kv_local, group_size)),
    )
    queries = queries.astype(jnp.bfloat16).reshape(req_here, NEW, kv_local, group_size, HD)
    new_keys = rotate(projected[:, :, group_size], flat_places[:, None])
    new_keys = new_keys.astype(jnp.bfloat16).reshape(req_here, NEW, kv_local, HD)
    new_values = (
        projected[:, :, group_size + 1].astype(jnp.bfloat16).reshape(req_here, NEW, kv_local, HD)
    )
    fresh_stats = new_stats(queries, new_keys, new_values)
    tail_len = TAIL
    entries = req_here * tail_len
    capacity = (entries + group_count - 2) // (group_count - 1)
    home_ids = jnp.broadcast_to(jnp.arange(KEEP, dtype=jnp.int32)[None, :], (req_here, KEEP))
    tail_ids = jnp.broadcast_to(
        KEEP + jnp.arange(tail_len, dtype=jnp.int32)[None, :], (req_here, tail_len)
    )
    home_pages = cache_pool[my_table[:, :KEEP]]
    tail_plan = rebalance_plan[:, KEEP:].reshape(group_count, entries)
    tail_table = page_table[:, KEEP:].reshape(group_count, entries)
    held_here = tail_plan == group_index
    held_rank = jnp.cumsum(held_here.astype(jnp.int32), axis=1) - 1
    picked = held_here[:, :, None] & (
        held_rank[:, :, None] == jnp.arange(capacity, dtype=jnp.int32)[None, None, :]
    )
    entry_ids = jnp.sum(
        jnp.where(picked, jnp.arange(entries, dtype=jnp.int32)[None, :, None], 0), axis=1
    )
    send_slots = jnp.take_along_axis(tail_table, entry_ids, axis=1)
    outgoing = cache_pool[send_slots]
    own_plan = my_plan[:, KEEP:].reshape(entries)
    at_group = own_plan[:, None] == jnp.arange(group_count, dtype=jnp.int32)[None, :]
    own_rank = jnp.sum(
        jnp.where(at_group, jnp.cumsum(at_group.astype(jnp.int32), axis=0) - 1, 0), axis=1
    )
    flat_index = own_plan * capacity + own_rank
    received = lax.all_to_all(outgoing, "req", split_axis=0, concat_axis=0, tiled=True)
    tail_pages = received.reshape(group_count * capacity, kv_local, -1)[flat_index].reshape(
        req_here, tail_len, kv_local, -1
    )
    dense_pages = jnp.concatenate([home_pages, tail_pages], axis=1)
    all_ids = jnp.concatenate([home_ids, tail_ids], axis=1)
    combined = fold_blocks(
        *page_stats(queries, dense_pages, page_valid(my_places, my_lengths, all_ids))
    )
    merged = join_pair(combined, fresh_stats)
    heads_out = merged[2] / merged[1][..., None]
    heads_out = jnp.transpose(heads_out, (0, 3, 1, 2, 4)).reshape(tok_rows, -1).astype(jnp.bfloat16)
    partial_value = jnp.dot(heads_out, output_proj, preferred_element_type=jnp.float32)
    return lax.psum_scatter(partial_value, "tp", scatter_dimension=1, tiled=True)


def solution(mesh):
    in_specs = (
        P("req", "tp"),
        P(),
        P(None, "tp", None),
        P("tp", None),
        P("req", "tp", None),
        P(),
        P(),
        P(),
        P(),
    )
    out_specs = P("req", "tp")
    return jax.shard_map(local, mesh=mesh, in_specs=in_specs, out_specs=out_specs, check_vma=False)
```

profile of v0, /device:TPU:6, one launch (start us, length us, event | category | flops | bytes accessed | tf_op | source)
XLA Modules:
  0.0 170.4 jit_solution(8499491559643690964)
XLA Ops:
  6.5 0.9 slice_compare_fusion
  7.4 0.1 copy.80
  7.5 0.1 eq.47
  7.6 0.7 slice.42
  8.3 0.2 reduce_window_sum.22
  8.5 0.1 select_reduce_fusion.1
  8.6 0.1 copy.82
  8.7 0.1 reshape.510
  9.0 0.8 gather_fusion.3
  9.8 0.1 gather.17
  10.0 0.1 copy.84
  10.1 0.1 reshape.494
  10.2 8.6 %gather_fusion.1 = bf16[64,20480]{1,0:T(8,128)(2,1)} fusion(bf16[94,20480]{1,0:T(8,128)(2,1)} %bitcast.127, s32[1024]{0:T(1024)S(1)} %pad_clamp_fusion.1), kind=kCustom, calls=%fused_computation.1 | custom fusion | bytes 5243136 | tf_op jit(solution)/shard_map/gather | solution.py:159
  18.8 4.8 %reshape.491 = bf16[32,2,1,20480]{3,1,0,2:T(2,128)(2,1)} reshape(bf16[64,20480]{1,0:T(8,128)(2,1)} %gather_fusion.1) | data formatting | bytes 5242880 | tf_op jit(solution)/shard_map/gather | solution.py:159
  23.6 7.8 %all-to-all-start = ((bf16[32,2,1,20480]{3,1,2,0:T(2,128)(2,1)}), bf16[32,2,1,20480]{3,1,2,0:T(2,128)(2,1)}, u32[]{:S(2)}, u32[]{:S(2)}) async-start(bf16[32,2,1,20480]{3,1,2,0:T(2,128)(2,1)} %bitcast.129), calls=%async_computation | async-start | bytes 5242880 | tf_op jit(solution)/shard_map/all_to_all | solution.py:166
  31.6 0.1 eq.51
  31.8 1.2 fusion.61
  33.1 29.3 %all_gather.3 = bf16[128,2560]{0,1:T(8,128)(2,1)S(1)} all-gather(bf16[128,320]{0,1:T(8,128)(2,1)S(1)} %copy-done.3), channel_id=1, replica_groups=mesh['req'=32,'tp'=8] {'tp'}, dimensions={1}, use_global_device_ids=true | all-gather | bytes 737280 | tf_op jit(solution)/shard_map/all_gather | solution.py:115
  62.4 0.4 fusion.10
  62.7 0.9 convolution_bitcast_fusion
  64.2 0.1 copy.94
  64.4 0.2 fusion.47
  64.5 0.1 copy.105
  64.6 0.1 copy.106
  64.8 0.2 fusion.36
  65.0 0.1 concatenate.47
  65.1 0.1 copy.90
  65.2 0.1 concatenate.48
  65.3 0.1 copy.91
  65.4 6.2 %gather_fusion = bf16[32,20480]{1,0:T(8,128)(2,1)} fusion(bf16[94,20480]{1,0:T(8,128)(2,1)} %bitcast.128, s32[1024]{0:T(1024)S(1)} %pad_clamp_fusion.2), kind=kCustom, calls=%fused_computation | custom fusion | bytes 2621568 | tf_op jit(solution)/shard_map/gather | solution.py:147
  71.7 4.5 %concatenate.44 = bf16[2,16,1,128,2,80]{5,4,3,1,0,2:T(2,128)(2,1)} reshape(bf16[32,20480]{1,0:T(8,128)(2,1)} %gather_fusion) | data formatting | bytes 2621440 | tf_op jit(solution)/shard_map/concatenate | solution.py:170
  76.2 5.9 %copy.87 = bf16[2,16,1,128,2,80]{3,5,1,0,4,2:T(8,128)(2,1)} copy(bf16[2,16,1,128,2,80]{5,4,3,1,0,2:T(2,128)(2,1)} %concatenate.44) | data formatting | bytes 2621440 | tf_op jit(solution)/shard_map/concatenate | solution.py:170
  82.1 0.2 select_reduce_fusion.2
  82.3 0.6 pad_clamp_fusion
  82.9 0.3 select_reduce_fusion
  83.5 1.2 fusion.9
  84.7 4.4 %reshape.500 = bf16[64,20480]{1,0:T(8,128)(2,1)} reshape(bf16[32,2,1,20480]{3,1,2,0:T(2,128)(2,1)} %all-to-all-done) | data formatting | bytes 5242880 | tf_op jit(solution)/shard_map/reshape | solution.py:167
  89.1 5.8 %gather_fusion.2 = bf16[32,20480]{1,0:T(8,128)(2,1)} fusion(bf16[64,20480]{1,0:T(8,128)(2,1)} %reshape.500, s32[1024]{0:T(1024)} %pad_clamp_fusion), kind=kCustom, calls=%fused_computation.2 | custom fusion | bytes 2621568 | tf_op jit(solution)/shard_map/gather | solution.py:167
  94.9 4.5 %concatenate.45 = bf16[2,16,1,128,2,80]{5,4,3,1,0,2:T(2,128)(2,1)} reshape(bf16[32,20480]{1,0:T(8,128)(2,1)} %gather_fusion.2) | data formatting | bytes 2621440 | tf_op jit(solution)/shard_map/concatenate | solution.py:170
  99.5 5.9 %copy.88 = bf16[2,16,1,128,2,80]{3,5,1,0,4,2:T(8,128)(2,1)} copy(bf16[2,16,1,128,2,80]{5,4,3,1,0,2:T(2,128)(2,1)} %concatenate.45) | data formatting | bytes 2621440 | tf_op jit(solution)/shard_map/concatenate | solution.py:170
  105.4 4.0 %fusion.3 = (f32[2,32,4,64]{3,2,1,0:T(4,128)S(1)}, f32[2,32,128,64,4]{2,3,4,1,0:T(8,128)S(1)}) fusion(pred[2,32,64,128]{3,2,1,0:T(8,128)(4,1)S(1)} %fusion.9, bf16[2,64,4,40]{3,1,2,0:T(8,128)(2,1)S(1)} %copy.91, bf16[2,64,4,40]{3,1,2,0:T(8,128)(2,1)S(1)} %copy.90, bf16[2,16,1,128,2,80]{3,5,1,0,4,2:T(8,128)(2,1)} %copy.87, ...), kind=kOutput, calls=%fused_computation.11 | convolution fusion | flops 344604672 | bytes 11681792 | tf_op jit(solution)/shard_map/rtkgd,rjkpd->rjkgtp/dot_general | solution.py:45
  109.4 5.8 %convert_reduce_fusion = (f32[2,32,4,64]{3,2,1,0:T(4,128)S(1)}, f32[2,4,64]{2,1,0:T(4,128)S(1)}) fusion(f32[2,32,4,64]{3,2,1,0:T(4,128)S(1)} %get-tuple-element.18, f32[2,32,128,64,4]{2,3,4,1,0:T(8,128)S(1)} %get-tuple-element.19, pred[2,32,64,128]{3,2,1,0:T(8,128)(4,1)S(1)} %fusion.9), kind=kLoop, calls=%fused_computation.9 | loop fusion | flops 16760320 | bytes 9046016 | tf_op jit(solution)/shard_map/reduce_sum | solution.py:53
  115.4 5.1 %multiply_reduce_fusion = f32[2,4,64,80]{3,2,1,0:T(8,128)S(1)} fusion(f32[2,32,4,64]{3,2,1,0:T(4,128)S(1)} %get-tuple-element.11, bf16[2,16,1,128,2,80]{3,5,1,0,4,2:T(8,128)(2,1)S(1)} %copy-done.2, bf16[2,16,1,128,2,80]{3,5,1,0,4,2:T(8,128)(2,1)S(1)} %copy-done.1, f32[2,32,128,64,4]{2,3,4,1,0:T(8,128)S(1)} %get-tuple-element.19, ...), kind=kOutput, calls=%fused_computation.10 | convolution fusion | flops 347168768 | bytes 11829248 | tf_op jit(solution)/shard_map/rjkgtp,rjkpd->rjkgtd/dot_general | solution.py:54
  120.5 0.3 fusion.24
  120.9 0.1 copy.96
  121.0 0.1 convert_element_type.92
  121.1 3.4 %fusion.62 = f32[128,2560]{0,1:T(8,128)} fusion(bf16[128,320]{1,0:T(8,128)(2,1)S(1)} %convert_element_type.92, bf16[320,2560]{1,0:T(8,128)(2,1)} %param.12), kind=kOutput, calls=%fused_computation.112 | convolution fusion | flops 209715200 | bytes 3031040 | tf_op jit(solution)/shard_map/dot_general | solution.py:178
  124.5 39.0 %reduce-scatter.2.cloned.1.call-done = f32[128,320]{0,1:T(8,128)} async-done(((f32[128,2560]{0,1:T(8,128)}), f32[128,320]{0,1:T(8,128)}) %reduce-scatter.2.cloned.1.call-update) | async-done | bytes 163856 | tf_op jit(solution)/shard_map/reduce_scatter | solution.py:179
  (54 shorter events, 1.6 us)
Async XLA Ops:
  6.5 56.2 %copy-start = (bf16[2560,1,480]{0,2,1:T(8,128)(2,1)S(1)}, bf16[2560,1,480]{0,2,1:T(8,128)(2,1)}, u32[]{:S(2)}) copy-start(bf16[2560,1,480]{0,2,1:T(8,128)(2,1)} %param.11) | copy-start | bytes 7372804
  23.6 7.9 %copy-start.4 = (s32[64,32]{0,1:T(8,128)S(1)}, s32[64,32]{0,1:T(8,128)}, u32[]{:S(2)}) copy-start(s32[64,32]{0,1:T(8,128)} %param.15) | copy-start | bytes 24580
  23.6 8.2 %copy-start.5 = (s32[64,32]{0,1:T(8,128)S(1)}, s32[64,32]{0,1:T(8,128)}, u32[]{:S(2)}) copy-start(s32[64,32]{0,1:T(8,128)} %param.14) | copy-start | bytes 24580
  23.6 9.5 %copy-start.3 = (bf16[128,320]{0,1:T(8,128)(2,1)S(1)}, bf16[128,320]{0,1:T(8,128)(2,1)}, u32[]{:S(2)}) copy-start(bf16[128,320]{0,1:T(8,128)(2,1)} %param.9) | copy-start | bytes 245764
  23.6 39.2 %copy-start.6 = (f32[2560]{0:T(1024)S(1)}, f32[2560]{0:T(1024)}, u32[]{:S(2)}) copy-start(f32[2560]{0:T(1024)} %param.10) | copy-start | bytes 30724
  23.6 61.1 %all-to-all-start = ((bf16[32,2,1,20480]{3,1,2,0:T(2,128)(2,1)}), bf16[32,2,1,20480]{3,1,2,0:T(2,128)(2,1)}, u32[]{:S(2)}, u32[]{:S(2)}) async-start(bf16[32,2,1,20480]{3,1,2,0:T(2,128)(2,1)} %bitcast.129), calls=%async_computation | async-start | bytes 5242880 | tf_op jit(solution)/shard_map/all_to_all | solution.py:166
  31.4 32.3 %copy-start.7 = (s32[64]{0:T(128)S(1)}, s32[64]{0:T(128)}, u32[]{:S(2)}) copy-start(s32[64]{0:T(128)} %param.16) | copy-start | bytes 772
  31.4 132.1 %reduce-scatter.2.cloned.1.call-start = ((), (), s32[]{:S(2)}) async-start(), calls=%async_computation.2 | async-start | bytes 1474560 | tf_op jit(solution)/shard_map/reduce_scatter | solution.py:179
  109.4 5.9 %copy-start.1 = (bf16[2,16,1,128,2,80]{3,5,1,0,4,2:T(8,128)(2,1)S(1)}, bf16[2,16,1,128,2,80]{3,5,1,0,4,2:T(8,128)(2,1)}, u32[]{:S(2)}) copy-start(bf16[2,16,1,128,2,80]{3,5,1,0,4,2:T(8,128)(2,1)} %copy.87) | copy-start | bytes 3932164
  109.4 5.9 %copy-start.2 = (bf16[2,16,1,128,2,80]{3,5,1,0,4,2:T(8,128)(2,1)S(1)}, bf16[2,16,1,128,2,80]{3,5,1,0,4,2:T(8,128)(2,1)}, u32[]{:S(2)}) copy-start(bf16[2,16,1,128,2,80]{3,5,1,0,4,2:T(8,128)(2,1)} %copy.88) | copy-start | bytes 3932164
Sparse Core Ops, SparseCore 0:
  124.7 38.8 reduce-scatter.1
where the time goes:
time: 171 us; the launch traced here: 170 us
  local copies, waits for them, and re-layouts  55 us (32%)
  waiting for transfers between devices  39 us (23%)
  blocking collectives  29.3 us (17%)
  matrix products  14.1 us (8%)
  between operations  13.7 us (8%)
  other arithmetic  11.5 us (7%)
  starting transfers between devices  7.84 us (5%)
    reduce_scatter x1, waiting for transfers between devices, local(): lax.psum_scatter(partial_value, 'tp', scatter_dimension=1, tiled=True)  39 us
    all_gather x1, blocking collectives, local(): gathered = lax.all_gather(activations, 'tp', axis=1, tiled=True)  29.3 us
    concatenate x4, local copies, waits for them, and re-layouts, local(): dense_pages = jnp.concatenate([home_pages, tail_pages], axis=1)  20.9 us
    gather x2, local copies, waits for them, and re-layouts, local(): outgoing = cache_pool[send_slots]  13.4 us
    all_to_all x1, starting transfers between devices, local(): lax.all_to_all(outgoing, 'req', split_axis=0, concat_axis=0, tiled=True)  7.8 us
    gather x1, local copies, waits for them, and re-layouts, local(): home_pages = cache_pool[my_table[:, :KEEP]]  6.23 us
    reduce_sum x1, other arithmetic, page_stats(): totals = jnp.sum(probabilities, axis=-1, dtype=jnp.float32)  5.84 us
    gather x1, local copies, waits for them, and re-layouts, local(): received.reshape(group_count * capacity, kv_local, -1)[flat_index]  5.8 us
  transfers between devices with their start and end apart: 2, of which 1 were waited for; matrix products, arithmetic and copies ran while one was open for 14% of the time, Pallas kernels for 0%

commit v1 on v0

v1 whole, which is shorter than its diff:
```python
import functools

import jax
import jax.numpy as jnp
import numpy as np
from jax import lax
from jax.experimental import pallas as pl
from jax.experimental.pallas import tpu as pltpu
from jax.sharding import PartitionSpec as P

MESH = pl.DeviceIdType.MESH
HD = 80
HALF = 40
WINDOW = 4096
PAGE = 128
KEEP = 16
TAIL = 16
NEW = 64
G = 4
GROUPS = 32
TP = 8
POOL = 94
D = 2560
ROWS = 32
WIDTH = 640
XB = 320
EPSILON = 1e-05
LOG_THETA = 9.210340371976184
MASKED = -1e30
SCALE = HD ** (-0.5) * 1.4426950408889634
KEY_TILE = ((0, 128, 0), (128, 128, 32), (256, 256, 64), (384, 256, 96))
VAL_TILE = ((0, 256, 80), (128, 256, 112), (384, 128, 16), (512, 128, 48))
OFFSETS = [(x, y, c) for x in range(4) for y in range(4) for c in range(2) if (x, y, c) != (0, 0, 0)]
np.random.RandomState(0).shuffle(OFFSETS)


STATED = (2, 0, 0)


def mm(a, b, contract):
    return lax.dot_general(a, b, (contract, ((), ())), preferred_element_type=jnp.float32)


def iota(shape, dim):
    return lax.broadcasted_iota(jnp.int32, shape, dim)


def kernel(
    rounds,
    x_hbm, gain_ref, w_hbm, wo_hbm, pool_hbm, table_ref, plan_ref, lens_ref, lens_s,
    out_ref,
    xf, pool, w, gb, wo, wot, gs, send, recv, xh, xt, qs, kn, vn, sc, stat, acc, hs, ht, rsend, rrecv, idx_v, idx,
    load_sem, page_ss, page_rs, ag_ss, ag_rs, rs_ss, rs_rs,
):
    me = lax.axis_index("req")
    z = lax.axis_index("tp")
    mx, my, mc = me // 8, (me // 2) % 4, me % 2
    zr, zl = lax.rem(z + 1, TP), lax.rem(z + TP - 1, TP)
    f32, bf16 = jnp.float32, jnp.bfloat16

    def peer(o):
        return ((mx + o[0]) % 4) * 8 + ((my + o[1]) % 4) * 2 + (mc + o[2]) % 2

    own = pl.ds(pl.multiple_of(z * XB, 64), XB)
    loads = [
        pltpu.make_async_copy(x_hbm, xf.at[own], load_sem.at[0]),
        pltpu.make_async_copy(pool_hbm, pool, load_sem.at[1]),
        pltpu.make_async_copy(w_hbm, w, load_sem.at[2]),
        pltpu.make_async_copy(wo_hbm, wo, load_sem.at[3]),
    ]
    for c in loads:
        c.start()
    barrier = pltpu.get_barrier_semaphore()
    for o in OFFSETS:
        pl.semaphore_signal(barrier, inc=1, device_id={"req": peer(o)}, device_id_type=MESH)
    for n in (zl, zr):
        pl.semaphore_signal(barrier, inc=1, device_id={"tp": n}, device_id_type=MESH)

    plan = plan_ref[KEEP:, :]
    table = table_ref[KEEP:, :]
    page_pos = (iota((TAIL, 64), 0) + KEEP) * PAGE
    held = (plan == me) & (page_pos < lens_ref[...])
    held_f = held.astype(f32)
    below = (iota((TAIL, TAIL), 0) > iota((TAIL, TAIL), 1)).astype(f32)
    rank = mm(below, held_f, ((1,), (0,)))
    count = mm(jnp.ones((8, TAIL), f32), held_f, ((1,), (0,)))
    r0, r1 = iota((64, 64), 0), iota((64, 64), 1)
    before = ((r1 % 2 == 1) & (r0 == r1 - 1)).astype(f32)
    rank = rank + mm(count, before, ((1,), (0,)))[0:1, :]
    slot_f = (table + 1).astype(f32)
    pair = (iota((GROUPS, 64), 0) == iota((GROUPS, 64), 1) // 2).astype(f32)
    sels = []
    for c in range(2):
        value = jnp.where(held & (rank == c), slot_f, 0.0)
        by_req = mm(value, jnp.ones((TAIL, 128), f32), ((0,), (0,)))
        col = mm(pair, by_req, ((1,), (0,)))[:, :POOL]
        sels.append((col == (iota((GROUPS, POOL), 1) + 1).astype(f32)).astype(bf16))
    tab = table_ref[:KEEP, :].astype(f32)
    lane = iota((KEEP, 64), 1)
    for a in range(2):
        col = jnp.sum(jnp.where(lane == 2 * me + a, tab, 0.0), axis=1, keepdims=True)
        sels.append((col == iota((KEEP, POOL), 1).astype(f32)).astype(bf16))
    sel = jnp.concatenate(sels, axis=0)

    loads[0].wait()
    pl.semaphore_wait(barrier, len(OFFSETS) + 2)

    def ag(step, way):
        block = lax.rem(z - step + TP, TP) if way == 0 else lax.rem(z + step, TP)
        rows = pl.ds(pl.multiple_of(block * XB, 64), XB)
        return pltpu.make_async_remote_copy(
            src_ref=xf.at[rows], dst_ref=xf.at[rows],
            send_sem=ag_ss.at[way * 4 + step], recv_sem=ag_rs.at[way * 4 + step],
            device_id={"tp": zr if way == 0 else zl}, device_id_type=MESH,
        )

    ags = {}

    def ag_step(step):
        for way in range(2):
            if step:
                ags[step - 1, way].wait_recv()
            if way == 0 or step < 3:
                ags[step, way] = ag(step, way)
                ags[step, way].start()

    ag_step(0)
    loads[1].wait()

    def pick(n, carry):
        for u in range(4):
            i = n * 4 + u
            rows = mm(sel, pool[:, pl.ds(pl.multiple_of(i * WIDTH, 128), WIDTH)], ((1,), (0,)))
            for k in range(5):
                gs[k, pl.ds(pl.multiple_of(i * 64, 64), 64), :] = rows[:64, k * 128 : (k + 1) * 128]
            at = pl.ds(pl.multiple_of(i * KEEP, KEEP), KEEP)
            xh[0, at, :] = rows[64 : 64 + KEEP].astype(bf16)
            xh[1, at, :] = rows[64 + KEEP :].astype(bf16)
        return carry

    lax.fori_loop(0, ROWS // 4, pick, 0)
    ag_step(1)

    def slots(o):
        return 2 if rounds == 2 or o == STATED else 1

    copies = []
    for n, o in enumerate(OFFSETS):
        p = peer(o)
        for c in range(slots(o)):
            for k in range(5):
                send[p, c, :, k * 128 : (k + 1) * 128] = gs[k, pl.ds(c * GROUPS + p, ROWS, stride=64), :].astype(bf16)
        held_slots = pl.ds(0, slots(o))
        copy = pltpu.make_async_remote_copy(
            src_ref=send.at[p, held_slots], dst_ref=recv.at[me, held_slots],
            send_sem=page_ss.at[n], recv_sem=page_rs.at[n], device_id={"req": p}, device_id_type=MESH,
        )
        copy.start()
        copies.append(copy)
    ag_step(2)

    cols, oks = [], []
    for a in range(2):
        cols.append(jnp.sum(jnp.where(lane == 2 * me + a, plan.astype(f32), 0.0), axis=1, keepdims=True))
        inside = (page_pos < lens_ref[...]).astype(f32)
        oks.append(jnp.sum(jnp.where(lane == 2 * me + a, inside, 0.0), axis=1, keepdims=True))
    group_col, ok_col = jnp.concatenate(cols, axis=0), jnp.concatenate(oks, axis=0)
    e0, e1 = iota((2 * TAIL, 128), 0), iota((2 * TAIL, 128), 1)
    group_row = jnp.sum(jnp.where(e0 == e1, group_col, 0.0), axis=0, keepdims=True)
    ok_row = jnp.sum(jnp.where(e0 == e1, ok_col, 0.0), axis=0, keepdims=True)
    earlier = jnp.where((group_col == group_row) & (e0 < e1), ok_col, 0.0)
    where_row = group_row * 2.0 + ok_row * jnp.sum(earlier, axis=0, keepdims=True)
    idx_v[...] = jnp.broadcast_to(where_row, (8, 128)).astype(jnp.int32)
    idx_copy = pltpu.make_async_copy(idx_v, idx, load_sem.at[4])
    idx_copy.start()

    for i in range(20):
        gb[i * 128 : (i + 1) * 128, :] = jnp.transpose(jnp.broadcast_to(gain_ref[i : i + 1, :], (128, 128)))
    ag_step(3)
    loads[3].wait()
    for i in range(20):
        wot[i * 128 : (i + 1) * 128, :] = jnp.transpose(wo[:, i * 128 : (i + 1) * 128])
    loads[2].wait()
    ags[3, 0].wait_recv()

    xw = xf[...].astype(f32)
    rstd = lax.rsqrt(jnp.sum(xw * xw, axis=0, keepdims=True) * (1.0 / D) + EPSILON)
    normed = (xw * rstd * gb[...]).astype(bf16)
    proj = mm(w[...], normed, ((1,), (0,)))
    lens0, lens1 = lens_s[2 * me], lens_s[2 * me + 1]
    tok = iota((1, 2 * NEW), 1)
    places = jnp.where(tok < NEW, lens0 + tok, lens1 + tok - NEW).astype(f32)
    freq = jnp.exp(iota((HALF, 128), 0).astype(f32) * (-2.0 * LOG_THETA / HD))
    angle = freq * places
    cos, sin = jnp.cos(angle), jnp.sin(angle)

    def rotated(first):
        front, back = proj[first : first + HALF], proj[first + HALF : first + HD]
        full = jnp.concatenate([front * cos - back * sin, back * cos + front * sin], axis=0)
        return full.astype(bf16).astype(f32)

    def turned(values, offset, width):
        pieces = [values]
        if offset:
            pieces.insert(0, jnp.zeros((offset, 2 * NEW), f32))
        pieces.append(jnp.zeros((width - offset - HD, 2 * NEW), f32))
        return jnp.transpose(jnp.concatenate(pieces, axis=0)).astype(bf16)

    for g in range(G):
        q = rotated(g * HD)
        for m, (_, width, offset) in enumerate(KEY_TILE):
            qt = turned(q, offset, width)
            for a in range(2):
                qs[m, a, g * NEW : (g + 1) * NEW, :width] = qt[a * NEW : (a + 1) * NEW]
    kn[...] = turned(rotated(G * HD), 0, 128)
    vn[...] = turned(proj[(G + 1) * HD :].astype(bf16).astype(f32), 0, 128)

    t_col = iota((G * NEW, 1), 0) % NEW

    def attend(a, keys, pos_of, top0, with_window):
        length = lens_s[2 * me + a]
        cols = iota((1, 512), 1)
        top = top0
        for m, (first, width, _) in enumerate(KEY_TILE):
            s = mm(qs[m, a, :, :width], keys[:, first : first + width], ((1,), (1,)))
            rel = pos_of(cols) + m - length
            ok = rel < 0
            if with_window:
                ok = ok & (rel > t_col - WINDOW)
            s = jnp.where(ok, s, MASKED)
            sc[m] = s
            top = jnp.maximum(top, jnp.max(s, axis=1, keepdims=True))
        total = jnp.zeros((G * NEW, 1), f32)
        sums = jnp.zeros((G * NEW, 128), f32)
        for m, (first, width, offset) in enumerate(VAL_TILE):
            p = jnp.exp2((sc[m] - top) * SCALE)
            total = total + jnp.sum(p, axis=1, keepdims=True)
            o = mm(p.astype(bf16), keys[:, first : first + width], ((1,), (0,)))
            sums = sums + pltpu.roll(o, width - offset, 1)[:, :128]
        return top, total, sums

    def home(a, carry):
        at = pl.ds(pl.multiple_of(a * NEW, NEW), NEW)
        s = mm(qs[0, a, :, :128], kn[at, :], ((1,), (1,)))
        s = jnp.where(iota((G * NEW, NEW), 1) <= t_col, s, MASKED)
        top_new = jnp.max(s, axis=1, keepdims=True)
        top, total, sums = attend(
            a, xh.at[a], lambda col: (col % KEEP) * PAGE + (col // KEEP) * 4, top_new, True
        )
        p = jnp.exp2((s - top) * SCALE)
        stat[a, 0] = jnp.broadcast_to(top, (G * NEW, 128))
        stat[a, 1] = jnp.broadcast_to(total + jnp.sum(p, axis=1, keepdims=True), (G * NEW, 128))
        acc[a] = sums + mm(p.astype(bf16), vn[at, :], ((1,), (0,)))
        return carry

    lax.fori_loop(0, 2, home, 0)

    idx_copy.wait()
    for copy in copies:
        copy.wait_recv()

    def tail(a, carry):
        for j in range(TAIL):
            where = jnp.clip(idx[0, a * TAIL + j], 0, 2 * GROUPS - 1)
            xt[j * ROWS : (j + 1) * ROWS, :] = recv[where // 2, where % 2]
        old_top = stat[a, 0][:, :1]
        top, total, sums = attend(a, xt, lambda col: KEEP * PAGE + col * 4, old_top, False)
        weight = jnp.exp2((old_top - top) * SCALE)
        result = (acc[a] * weight + sums) / (stat[a, 1][:, :1] * weight + total)
        for g in range(G):
            hs[g, pl.ds(pl.multiple_of(a * NEW, NEW), NEW), :] = result[g * NEW : (g + 1) * NEW]
        return carry

    lax.fori_loop(0, 2, tail, 0)
    for g in range(G):
        ht[g * HD : (g + 1) * HD, :] = jnp.transpose(hs[g])[:HD].astype(bf16)

    def project(dest):
        rows = pl.ds(pl.multiple_of(dest * XB, 64), XB)
        return mm(wot[rows, :], ht[...], ((1,), (0,)))

    HB = XB // 2
    pending = {}
    for step in range(4):
        for way in range(2):
            hop = step if way == 0 else step - 1
            if hop < 0:
                continue
            dest = lax.rem(z + 4 - step, TP) if way == 0 else lax.rem(z + TP - 3 + hop, TP)
            mine = project(dest)
            for h in range(2):
                n = way * 8 + hop * 2 + h
                block = mine[h * HB : (h + 1) * HB]
                if hop:
                    pending[n - 2].wait_recv()
                    block = block + rrecv[n - 2].astype(f32)
                rsend[n] = block.astype(bf16)
                copy = pltpu.make_async_remote_copy(
                    src_ref=rsend.at[n], dst_ref=rrecv.at[n], send_sem=rs_ss.at[n], recv_sem=rs_rs.at[n],
                    device_id={"tp": zr if way == 0 else zl}, device_id_type=MESH,
                )
                copy.start()
                pending[n] = copy
    mine = project(z)
    for h in range(2):
        last = (6 + h, 8 + 4 + h)
        block = mine[h * HB : (h + 1) * HB]
        for n in last:
            pending[n].wait_recv()
            block = block + rrecv[n].astype(f32)
        out_ref[h * HB : (h + 1) * HB, :] = block

    for copy in list(ags.values()) + copies + list(pending.values()):
        copy.wait_send()


def second_round(plan_ref, lens_ref, out_ref):
    f32 = jnp.float32
    group = iota((GROUPS, 64), 0)
    held = jnp.zeros((GROUPS, 64), f32)
    for j in range(KEEP, KEEP + TAIL):
        held += ((plan_ref[j : j + 1, :] == group) & (lens_ref[...] > j * PAGE)).astype(f32)
    pair = (iota((64, GROUPS), 0) // 2 == iota((64, GROUPS), 1)).astype(f32)
    pages = mm(held, pair, ((1,), (0,)))
    r0, r1 = iota((GROUPS, GROUPS), 0), iota((GROUPS, GROUPS), 1)
    pages = jnp.where(r0 == (r1 + GROUPS // 2) % GROUPS, 0.0, pages)
    out_ref[0] = (jnp.max(pages) > 1.5).astype(jnp.int32)


def layer(rounds, *operands):
    any_space = pl.BlockSpec(memory_space=pl.ANY)
    vmem = pl.BlockSpec(memory_space=pltpu.VMEM)
    smem = pl.BlockSpec(memory_space=pltpu.SMEM)
    f32, bf16 = jnp.float32, jnp.bfloat16
    dma = pltpu.SemaphoreType.DMA
    return pl.pallas_call(
        functools.partial(kernel, rounds),
        out_shape=jax.ShapeDtypeStruct((XB, 128), f32),
        in_specs=[any_space, vmem, any_space, any_space, any_space, vmem, vmem, vmem, smem],
        out_specs=vmem,
        scratch_shapes=[
            pltpu.VMEM((D, 128), bf16),
            pltpu.VMEM((POOL, ROWS * WIDTH), bf16),
            pltpu.VMEM((480, D), bf16),
            pltpu.VMEM((D, 128), f32),
            pltpu.VMEM((XB, D), bf16),
            pltpu.VMEM((D, XB), bf16),
            pltpu.VMEM((5, ROWS * 64, 128), f32),
            pltpu.VMEM((GROUPS, 2, ROWS, WIDTH), bf16),
            pltpu.VMEM((GROUPS, 2, ROWS, WIDTH), bf16),
            pltpu.VMEM((2, 512, WIDTH), bf16),
            pltpu.VMEM((512, WIDTH), bf16),
            pltpu.VMEM((4, 2, G * NEW, 256), bf16),
            pltpu.VMEM((128, 128), bf16),
            pltpu.VMEM((128, 128), bf16),
            pltpu.VMEM((4, G * NEW, 512), f32),
            pltpu.VMEM((2, 2, G * NEW, 128), f32),
            pltpu.VMEM((2, G * NEW, 128), f32),
            pltpu.VMEM((G, 128, 128), f32),
            pltpu.VMEM((XB, 128), bf16),
            pltpu.VMEM((16, XB // 2, 128), bf16),
            pltpu.VMEM((16, XB // 2, 128), bf16),
            pltpu.VMEM((8, 128), jnp.int32),
            pltpu.SMEM((8, 128), jnp.int32),
            dma((5,)), dma((31,)), dma((31,)), dma((8,)), dma((8,)), dma((16,)), dma((16,)),
        ],
        compiler_params=pltpu.CompilerParams(
            collective_id=rounds, has_side_effects=True, vmem_limit_bytes=60 * 2**20
        ),
        name=f"paged_prefill_{rounds}",
    )(*operands)


def local(activations, norm_gain, input_proj, output_proj, cache_pool, page_table, rebalance_plan, cached_lengths, token_positions):
    vmem = pl.BlockSpec(memory_space=pltpu.VMEM)
    plan, lens = rebalance_plan.T, cached_lengths.reshape(1, 64)
    more = pl.pallas_call(
        second_round,
        out_shape=jax.ShapeDtypeStruct((1,), jnp.int32),
        in_specs=[vmem, vmem],
        out_specs=pl.BlockSpec(memory_space=pltpu.SMEM),
        name="second_round",
    )(plan, lens)
    out = lax.cond(
        more[0] > 0,
        functools.partial(layer, 2),
        functools.partial(layer, 1),
        activations.T,
        norm_gain.reshape(20, 128),
        jnp.transpose(input_proj, (1, 2, 0)).reshape(480, D),
        output_proj,
        cache_pool.reshape(POOL, ROWS * WIDTH),
        page_table.T,
        plan,
        lens,
        cached_lengths,
    )
    return out.T


def solution(mesh):
    in_specs = (
        P("req", "tp"), P(), P(None, "tp", None), P("tp", None), P("req", "tp", None), P(), P(), P(), P(),
    )
    return jax.shard_map(local, mesh=mesh, in_specs=in_specs, out_specs=P("req", "tp"), check_vma=False)
```

time: 171 us -> 53.8 us (0.31)
  the two profiles are of different devices: /device:TPU:6 before, /device:TPU:34 now
where the time goes in v1:
time: 53.8 us; the launch traced here: 53.6 us
  Pallas kernels  52 us (97%)
  local copies, waits for them, and re-layouts  0.67 us (1%)
  between operations  0.67 us (1%)
    pallas_call x1, Pallas kernels, layer(): pl.pallas_call(functools.partial(kernel, rounds), out_shape=jax.ShapeDtyp...  50.5 us
    pallas_call x1, Pallas kernels, local(): pl.pallas_call(second_round, out_shape=jax.ShapeDtypeStruct((1,), jnp.int...  1.52 us

profile of v1, /device:TPU:34, one launch (start us, length us, event | category | flops | bytes accessed | tf_op | source)
XLA Modules:
  0.0 53.6 jit_solution(15820797675340438561)
XLA Ops:
  0.0 1.5 %second_round.1 = s32[1]{0:T(128)} custom-call(s32[32,64]{1,0:T(8,128)} %bitcast.18, s32[1,64]{1,0:T(1,128)} %bitcast.25), custom_call_target="tpu_custom_call" | custom-call | tf_op jit(solution)/shard_map/second_round/pallas_call | solution.py:377
  2.2 50.7 %conditional.1 = (f32[320,128]{1,0:T(8,128)S(1)}) conditional(s32[]{:T(128)} %bitcast.2, (bf16[320,128]{1,0:T(8,128)(2,1)}, f32[20,128]{1,0:T(8,128)}, bf16[480,2560]{1,0:T(8,128)(2,1)}, bf16[320,2560]{1,0:T(8,128)(2,1)}, bf16[94,20480]{1,0:T(8,128)(2,1)}, /*index=5*/s32[32,64]{1,0:T(8,128)}, s32[32,64]{1,0:T(8,128)}, s32[1,64]{1,0:T(1,128)}, ...), branch_computations={%region_0.0_spmd, %region_1.0_spmd} | conditional | bytes 8 | solution.py:384
  2.2 50.5 %paged_prefill_1.1 = f32[320,128]{1,0:T(8,128)S(1)} custom-call(bf16[320,128]{1,0:T(8,128)(2,1)} %get-tuple-element.44.x_hbm, f32[20,128]{1,0:T(8,128)} %get-tuple-element.45.gain_ref, bf16[480,2560]{1,0:T(8,128)(2,1)} %get-tuple-element.46.w_hbm, bf16[320,2560]{1,0:T(8,128)(2,1)} %get-tuple-element.47.wo_hbm, bf16[94,20480]{1,0:T(8,128)(2,1)} %get-tuple-element.48.pool_hbm, ...), custom_call_target="tpu_custom_call" | custom-call | tf_op jit(solution)/shard_map/cond/branch_0_fun/paged_prefill_1/pallas_call | solution.py:336
  52.9 0.7 %copy.12 = f32[128,320]{0,1:T(8,128)} copy(f32[128,320]{0,1:T(8,128)S(1)} %bitcast.15) | data formatting | bytes 327680

commit v2 on v1

--- a/solution.py
+++ b/solution.py
@@ -2,7 +2,6 @@
 
 import jax
 import jax.numpy as jnp
-import numpy as np
 from jax import lax
 from jax.experimental import pallas as pl
 from jax.experimental.pallas import tpu as pltpu
@@ -31,9 +30,8 @@
 KEY_TILE = ((0, 128, 0), (128, 128, 32), (256, 256, 64), (384, 256, 96))
 VAL_TILE = ((0, 256, 80), (128, 256, 112), (384, 128, 16), (512, 128, 48))
 OFFSETS = [(x, y, c) for x in range(4) for y in range(4) for c in range(2) if (x, y, c) != (0, 0, 0)]
-np.random.RandomState(0).shuffle(OFFSETS)
-
-
+OFFSETS.sort(key=lambda o: -min(o[0], 4 - o[0]) - min(o[1], 4 - o[1]))
+Z_STEPS = (4, 3, 5, 2, 6, 1, 7)
 STATED = (2, 0, 0)
 
 
@@ -48,14 +46,13 @@
 def kernel(
     rounds,
     x_hbm, gain_ref, w_hbm, wo_hbm, pool_hbm, table_ref, plan_ref, lens_ref, lens_s,
-    out_ref,
+    out_ref, more_ref,
     xf, pool, w, gb, wo, wot, gs, send, recv, xh, xt, qs, kn, vn, sc, stat, acc, hs, ht, rsend, rrecv, idx_v, idx,
     load_sem, page_ss, page_rs, ag_ss, ag_rs, rs_ss, rs_rs,
 ):
     me = lax.axis_index("req")
     z = lax.axis_index("tp")
     mx, my, mc = me // 8, (me // 2) % 4, me % 2
-    zr, zl = lax.rem(z + 1, TP), lax.rem(z + TP - 1, TP)
     f32, bf16 = jnp.float32, jnp.bfloat16
 
     def peer(o):
@@ -73,8 +70,8 @@
     barrier = pltpu.get_barrier_semaphore()
     for o in OFFSETS:
         pl.semaphore_signal(barrier, inc=1, device_id={"req": peer(o)}, device_id_type=MESH)
-    for n in (zl, zr):
-        pl.semaphore_signal(barrier, inc=1, device_id={"tp": n}, device_id_type=MESH)
+    for k in Z_STEPS:
+        pl.semaphore_signal(barrier, inc=1, device_id={"tp": lax.rem(z + k, TP)}, device_id_type=MESH)
 
     plan = plan_ref[KEEP:, :]
     table = table_ref[KEEP:, :]
@@ -89,75 +86,84 @@
     rank = rank + mm(count, before, ((1,), (0,)))[0:1, :]
     slot_f = (table + 1).astype(f32)
     pair = (iota((GROUPS, 64), 0) == iota((GROUPS, 64), 1) // 2).astype(f32)
+    stated = peer(STATED)
     sels = []
     for c in range(2):
         value = jnp.where(held & (rank == c), slot_f, 0.0)
         by_req = mm(value, jnp.ones((TAIL, 128), f32), ((0,), (0,)))
         col = mm(pair, by_req, ((1,), (0,)))[:, :POOL]
-        sels.append((col == (iota((GROUPS, POOL), 1) + 1).astype(f32)).astype(bf16))
+        if c == 1 and rounds == 1:
+            col = jnp.sum(jnp.where(iota((GROUPS, POOL), 0) == stated, col, 0.0), axis=0, keepdims=True)
+            col = jnp.broadcast_to(col, (8, POOL))
+        sels.append((col == (iota(col.shape, 1) + 1).astype(f32)).astype(bf16))
+    sel = jnp.concatenate(sels, axis=0)
+    out_rows = sel.shape[0]
+
+    loads[0].wait()
+    pl.semaphore_wait(barrier, len(OFFSETS) + len(Z_STEPS))
+
+    ags = []
+    for k in Z_STEPS:
+        copy = pltpu.make_async_remote_copy(
+            src_ref=xf.at[own], dst_ref=xf.at[own], send_sem=ag_ss.at[k], recv_sem=ag_rs.at[k],
+            device_id={"tp": lax.rem(z + k, TP)}, device_id_type=MESH,
+        )
+        copy.start()
+        ags.append(copy)
+    loads[1].wait()
+
+    def slots(o):
+        return 2 if rounds == 2 or o == STATED else 1
+
+    copies = []
+    half_rows = ROWS // 2
+    for half in range(2):
+
+        def pick(n, carry, half=half):
+            for u in range(4):
+                i = half * half_rows + n * 4 + u
+                rows = mm(sel, pool[:, pl.ds(pl.multiple_of(i * WIDTH, 128), WIDTH)], ((1,), (0,)))
+                for k in range(5):
+                    gs[k, pl.ds(pl.multiple_of(i * out_rows, 8), out_rows), :] = rows[:, k * 128 : (k + 1) * 128]
+            return carry
+
+        lax.fori_loop(0, half_rows // 4, pick, 0)
+        at = pl.ds(half * half_rows, half_rows)
+        for n, o in enumerate(OFFSETS):
+            p = peer(o)
+            for c in range(slots(o)):
+                row = half * half_rows * out_rows + c * GROUPS + (0 if c == 1 and rounds == 1 else p)
+                for k in range(5):
+                    send[p, c, at, k * 128 : (k + 1) * 128] = gs[
+                        k, pl.ds(row, half_rows, stride=out_rows), :
+                    ].astype(bf16)
+            held_slots = pl.ds(0, slots(o))
+            copy = pltpu.make_async_remote_copy(
+                src_ref=send.at[p, held_slots, at], dst_ref=recv.at[me, held_slots, at],
+                send_sem=page_ss.at[half, n], recv_sem=page_rs.at[half, n],
+                device_id={"req": p}, device_id_type=MESH,
+            )
+            copy.start()
+            copies.append(copy)
+
     tab = table_ref[:KEEP, :].astype(f32)
     lane = iota((KEEP, 64), 1)
+    homes = []
     for a in range(2):
         col = jnp.sum(jnp.where(lane == 2 * me + a, tab, 0.0), axis=1, keepdims=True)
-        sels.append((col == iota((KEEP, POOL), 1).astype(f32)).astype(bf16))
-    sel = jnp.concatenate(sels, axis=0)
-
-    loads[0].wait()
-    pl.semaphore_wait(barrier, len(OFFSETS) + 2)
-
-    def ag(step, way):
-        block = lax.rem(z - step + TP, TP) if way == 0 else lax.rem(z + step, TP)
-        rows = pl.ds(pl.multiple_of(block * XB, 64), XB)
-        return pltpu.make_async_remote_copy(
-            src_ref=xf.at[rows], dst_ref=xf.at[rows],
-            send_sem=ag_ss.at[way * 4 + step], recv_sem=ag_rs.at[way * 4 + step],
-            device_id={"tp": zr if way == 0 else zl}, device_id_type=MESH,
-        )
-
-    ags = {}
-
-    def ag_step(step):
-        for way in range(2):
-            if step:
-                ags[step - 1, way].wait_recv()
-            if way == 0 or step < 3:
-                ags[step, way] = ag(step, way)
-                ags[step, way].start()
-
-    ag_step(0)
-    loads[1].wait()
-
-    def pick(n, carry):
+        homes.append((col == iota((KEEP, POOL), 1).astype(f32)).astype(bf16))
+    home_sel = jnp.concatenate(homes, axis=0)
+
+    def pick_home(n, carry):
         for u in range(4):
             i = n * 4 + u
-            rows = mm(sel, pool[:, pl.ds(pl.multiple_of(i * WIDTH, 128), WIDTH)], ((1,), (0,)))
-            for k in range(5):
-                gs[k, pl.ds(pl.multiple_of(i * 64, 64), 64), :] = rows[:64, k * 128 : (k + 1) * 128]
+            rows = mm(home_sel, pool[:, pl.ds(pl.multiple_of(i * WIDTH, 128), WIDTH)], ((1,), (0,))).astype(bf16)
             at = pl.ds(pl.multiple_of(i * KEEP, KEEP), KEEP)
-            xh[0, at, :] = rows[64 : 64 + KEEP].astype(bf16)
-            xh[1, at, :] = rows[64 + KEEP :].astype(bf16)
+            xh[0, at, :] = rows[:KEEP]
+            xh[1, at, :] = rows[KEEP:]
         return carry
 
-    lax.fori_loop(0, ROWS // 4, pick, 0)
-    ag_step(1)
-
-    def slots(o):
-        return 2 if rounds == 2 or o == STATED else 1
-
-    copies = []
-    for n, o in enumerate(OFFSETS):
-        p = peer(o)
-        for c in range(slots(o)):
-            for k in range(5):
-                send[p, c, :, k * 128 : (k + 1) * 128] = gs[k, pl.ds(c * GROUPS + p, ROWS, stride=64), :].astype(bf16)
-        held_slots = pl.ds(0, slots(o))
-        copy = pltpu.make_async_remote_copy(
-            src_ref=send.at[p, held_slots], dst_ref=recv.at[me, held_slots],
-            send_sem=page_ss.at[n], recv_sem=page_rs.at[n], device_id={"req": p}, device_id_type=MESH,
-        )
-        copy.start()
-        copies.append(copy)
-    ag_step(2)
+    lax.fori_loop(0, ROWS // 4, pick_home, 0)
 
     cols, oks = [], []
     for a in range(2):
@@ -176,12 +182,21 @@
 
     for i in range(20):
         gb[i * 128 : (i + 1) * 128, :] = jnp.transpose(jnp.broadcast_to(gain_ref[i : i + 1, :], (128, 128)))
-    ag_step(3)
     loads[3].wait()
     for i in range(20):
         wot[i * 128 : (i + 1) * 128, :] = jnp.transpose(wo[:, i * 128 : (i + 1) * 128])
+    group = iota((GROUPS, 64), 0)
+    owed = jnp.zeros((GROUPS, 64), f32)
+    for j in range(KEEP, KEEP + TAIL):
+        owed += ((plan_ref[j : j + 1, :] == group) & (lens_ref[...] > j * PAGE)).astype(f32)
+    owed = mm(owed, (iota((64, GROUPS), 0) // 2 == iota((64, GROUPS), 1)).astype(f32), ((1,), (0,)))
+    g0, g1 = iota((GROUPS, GROUPS), 0), iota((GROUPS, GROUPS), 1)
+    owed = jnp.where(g0 == (g1 + GROUPS // 2) % GROUPS, 0.0, owed)
+    more_ref[0] = (jnp.max(owed) > 1.5).astype(jnp.int32)
+
     loads[2].wait()
-    ags[3, 0].wait_recv()
+    for copy in ags:
+        copy.wait_recv()
 
     xw = xf[...].astype(f32)
     rstd = lax.rsqrt(jnp.sum(xw * xw, axis=0, keepdims=True) * (1.0 / D) + EPSILON)
@@ -279,52 +294,24 @@
         rows = pl.ds(pl.multiple_of(dest * XB, 64), XB)
         return mm(wot[rows, :], ht[...], ((1,), (0,)))
 
-    HB = XB // 2
-    pending = {}
-    for step in range(4):
-        for way in range(2):
-            hop = step if way == 0 else step - 1
-            if hop < 0:
-                continue
-            dest = lax.rem(z + 4 - step, TP) if way == 0 else lax.rem(z + TP - 3 + hop, TP)
-            mine = project(dest)
-            for h in range(2):
-                n = way * 8 + hop * 2 + h
-                block = mine[h * HB : (h + 1) * HB]
-                if hop:
-                    pending[n - 2].wait_recv()
-                    block = block + rrecv[n - 2].astype(f32)
-                rsend[n] = block.astype(bf16)
-                copy = pltpu.make_async_remote_copy(
-                    src_ref=rsend.at[n], dst_ref=rrecv.at[n], send_sem=rs_ss.at[n], recv_sem=rs_rs.at[n],
-                    device_id={"tp": zr if way == 0 else zl}, device_id_type=MESH,
-                )
-                copy.start()
-                pending[n] = copy
-    mine = project(z)
-    for h in range(2):
-        last = (6 + h, 8 + 4 + h)
-        block = mine[h * HB : (h + 1) * HB]
-        for n in last:
-            pending[n].wait_recv()
-            block = block + rrecv[n].astype(f32)
-        out_ref[h * HB : (h + 1) * HB, :] = block
-
-    for copy in list(ags.values()) + copies + list(pending.values()):
+    sums = []
+    for k in Z_STEPS:
+        dest = lax.rem(z + k, TP)
+        rsend[k] = project(dest).astype(bf16)
+        copy = pltpu.make_async_remote_copy(
+            src_ref=rsend.at[k], dst_ref=rrecv.at[k], send_sem=rs_ss.at[k], recv_sem=rs_rs.at[k],
+            device_id={"tp": dest}, device_id_type=MESH,
+        )
+        copy.start()
+        sums.append(copy)
+    total = project(z)
+    for k, copy in reversed(list(zip(Z_STEPS, sums))):
+        copy.wait_recv()
+        total = total + rrecv[k].astype(f32)
+    out_ref[...] = total
+
+    for copy in ags + copies + sums:
         copy.wait_send()
-
-
-def second_round(plan_ref, lens_ref, out_ref):
-    f32 = jnp.float32
-    group = iota((GROUPS, 64), 0)
-    held = jnp.zeros((GROUPS, 64), f32)
-    for j in range(KEEP, KEEP + TAIL):
-        held += ((plan_ref[j : j + 1, :] == group) & (lens_ref[...] > j * PAGE)).astype(f32)
-    pair = (iota((64, GROUPS), 0) // 2 == iota((64, GROUPS), 1)).astype(f32)
-    pages = mm(held, pair, ((1,), (0,)))
-    r0, r1 = iota((GROUPS, GROUPS), 0), iota((GROUPS, GROUPS), 1)
-    pages = jnp.where(r0 == (r1 + GROUPS // 2) % GROUPS, 0.0, pages)
-    out_ref[0] = (jnp.max(pages) > 1.5).astype(jnp.int32)
 
 
 def layer(rounds, *operands):
@@ -335,9 +322,9 @@
     dma = pltpu.SemaphoreType.DMA
     return pl.pallas_call(
         functools.partial(kernel, rounds),
-        out_shape=jax.ShapeDtypeStruct((XB, 128), f32),
+        out_shape=(jax.ShapeDtypeStruct((XB, 128), f32), jax.ShapeDtypeStruct((1,), jnp.int32)),
         in_specs=[any_space, vmem, any_space, any_space, any_space, vmem, vmem, vmem, smem],
-        out_specs=vmem,
+        out_specs=(vmem, smem),
         scratch_shapes=[
             pltpu.VMEM((D, 128), bf16),
             pltpu.VMEM((POOL, ROWS * WIDTH), bf16),
@@ -358,11 +345,11 @@
             pltpu.VMEM((2, G * NEW, 128), f32),
             pltpu.VMEM((G, 128, 128), f32),
             pltpu.VMEM((XB, 128), bf16),
-            pltpu.VMEM((16, XB // 2, 128), bf16),
-            pltpu.VMEM((16, XB // 2, 128), bf16),
+            pltpu.VMEM((TP, XB, 128), bf16),
+            pltpu.VMEM((TP, XB, 128), bf16),
             pltpu.VMEM((8, 128), jnp.int32),
             pltpu.SMEM((8, 128), jnp.int32),
-            dma((5,)), dma((31,)), dma((31,)), dma((8,)), dma((8,)), dma((16,)), dma((16,)),
+            dma((5,)), dma((2, 31)), dma((2, 31)), dma((TP,)), dma((TP,)), dma((TP,)), dma((TP,)),
         ],
         compiler_params=pltpu.CompilerParams(
             collective_id=rounds, has_side_effects=True, vmem_limit_bytes=60 * 2**20
@@ -372,29 +359,19 @@
 
 
 def local(activations, norm_gain, input_proj, output_proj, cache_pool, page_table, rebalance_plan, cached_lengths, token_positions):
-    vmem = pl.BlockSpec(memory_space=pltpu.VMEM)
-    plan, lens = rebalance_plan.T, cached_lengths.reshape(1, 64)
-    more = pl.pallas_call(
-        second_round,
-        out_shape=jax.ShapeDtypeStruct((1,), jnp.int32),
-        in_specs=[vmem, vmem],
-        out_specs=pl.BlockSpec(memory_space=pltpu.SMEM),
-        name="second_round",
-    )(plan, lens)
-    out = lax.cond(
-        more[0] > 0,
-        functools.partial(layer, 2),
-        functools.partial(layer, 1),
+    operands = (
         activations.T,
         norm_gain.reshape(20, 128),
         jnp.transpose(input_proj, (1, 2, 0)).reshape(480, D),
         output_proj,
         cache_pool.reshape(POOL, ROWS * WIDTH),
         page_table.T,
-        plan,
-        lens,
+        rebalance_plan.T,
+        cached_lengths.reshape(1, 64),
         cached_lengths,
     )
+    out, more = layer(1, *operands)
+    out = lax.cond(more[0] > 0, lambda first, *rest: layer(2, *rest)[0], lambda first, *rest: first, out, *operands)
     return out.T
 
 

time: 53.8 us -> 55.9 us (1.039)
  the two profiles are of different devices: /device:TPU:34 before, /device:TPU:1 now
where the time goes in v2:
time: 55.9 us; the launch traced here: 55.8 us
  Pallas kernels  53.3 us (95%)
  local copies, waits for them, and re-layouts  1.61 us (3%)
  between operations  0.61 us (1%)
    pallas_call x1, Pallas kernels, layer(): pl.pallas_call(functools.partial(kernel, rounds), out_shape=(jax.ShapeDty...  53.3 us
    unnamed x9, local copies, waits for them, and re-layouts  1.61 us

profile of v2, /device:TPU:1, one launch (start us, length us, event | category | flops | bytes accessed | tf_op | source)
XLA Modules:
  0.0 55.8 jit_solution(16417770415729785971)
XLA Ops:
  0.0 0.0 copy-start
  0.0 0.0 copy-start.1
  0.0 0.0 copy-start.2
  0.0 0.0 copy-start.3
  0.0 53.3 %paged_prefill_1.1 = (f32[320,128]{1,0:T(8,128)}, s32[1]{0:T(128)}) custom-call(bf16[320,128]{1,0:T(8,128)(2,1)} %bitcast.15, f32[20,128]{1,0:T(8,128)} %bitcast.22, bf16[480,2560]{1,0:T(8,128)(2,1)} %bitcast.13, bf16[320,2560]{1,0:T(8,128)(2,1)} %wo_hbm.1, bf16[94,20480]{1,0:T(8,128)(2,1)} %bitcast.11, s32[32,64]{1,0:T(8,128)} %bitcast.18, ...), custom_call_target="tpu_custom_call" | custom-call | tf_op jit(solution)/shard_map/paged_prefill_1/pallas_call | solution.py:323
  53.9 0.0 copy-done
  53.9 0.0 copy-done.1
  53.9 0.0 copy-done.2
  53.9 0.0 copy-done.3
  53.9 0.2 conditional.1
  54.2 1.6 %copy.12 = f32[128,320]{0,1:T(8,128)} copy(f32[128,320]{0,1:T(8,128)} %bitcast.17) | data formatting | bytes 327680
Async XLA Ops:
  0.0 53.9 %copy-start = (bf16[2560,1,480]{0,2,1:T(8,128)(2,1)S(1)}, bf16[2560,1,480]{0,2,1:T(8,128)(2,1)}, u32[]{:S(2)}) copy-start(bf16[2560,1,480]{0,2,1:T(8,128)(2,1)} %param.13) | copy-start | bytes 7372804
  0.0 53.9 %copy-start.1 = (bf16[320,2560]{1,0:T(8,128)(2,1)S(1)}, bf16[320,2560]{1,0:T(8,128)(2,1)}, u32[]{:S(2)}) copy-start(bf16[320,2560]{1,0:T(8,128)(2,1)} %wo_hbm.1) | copy-start | bytes 4915204
  0.0 53.9 %copy-start.2 = (s32[64,32]{0,1:T(8,128)S(1)}, s32[64,32]{0,1:T(8,128)}, u32[]{:S(2)}) copy-start(s32[64,32]{0,1:T(8,128)} %param.16) | copy-start | bytes 24580
  0.0 53.9 %copy-start.3 = (s32[64,32]{0,1:T(8,128)S(1)}, s32[64,32]{0,1:T(8,128)}, u32[]{:S(2)}) copy-start(s32[64,32]{0,1:T(8,128)} %param.17) | copy-start | bytes 24580

commit v3 on v2

v3 whole, which is shorter than its diff:
```python
import functools

import jax
import jax.numpy as jnp
from jax import lax
from jax.experimental import pallas as pl
from jax.experimental.pallas import tpu as pltpu
from jax.sharding import PartitionSpec as P

MESH = pl.DeviceIdType.MESH
HD = 80
HALF = 40
WINDOW = 4096
PAGE = 128
KEEP = 16
TAIL = 16
NEW = 64
G = 4
GROUPS = 32
TP = 8
POOL = 94
D = 2560
ROWS = 32
WIDTH = 640
XB = 320
EPSILON = 1e-05
LOG_THETA = 9.210340371976184
MASKED = -1e30
SCALE = HD ** (-0.5) * 1.4426950408889634
STEP = 96
KEY_TILE = ((0, 128, 0, 0), (128, 128, 128, 160), (256, 256, 256, 320), (384, 256, 512, 608))
QUERY_LANES = 768
VAL_TILE = ((0, 256, 80), (128, 256, 112), (384, 128, 16), (512, 128, 48))
OFFSETS = [(x, y, c) for x in range(4) for y in range(4) for c in range(2) if (x, y, c) != (0, 0, 0)]
OFFSETS.sort(key=lambda o: -min(o[0], 4 - o[0]) - min(o[1], 4 - o[1]))
Z_STEPS = (4, 3, 5, 2, 6, 1, 7)
STATED = (2, 0, 0)


def mm(a, b, contract):
    return lax.dot_general(a, b, (contract, ((), ())), preferred_element_type=jnp.float32)


def iota(shape, dim):
    return lax.broadcasted_iota(jnp.int32, shape, dim)


def kernel(
    rounds,
    x_hbm, gain_ref, w_hbm, wo_hbm, pool_hbm, table_ref, plan_ref, lens_ref, lens_s,
    out_ref, more_ref,
    cos_sin, xf, pool, w, gb, wo, wot, pf, send, recv, xh, xt, qs, kn, vn, sc, stat, acc, hs, ht, part, rrecv, idx_v, idx,
    load_sem, page_ss, page_rs, ag_ss, ag_rs, rs_ss, rs_rs,
):
    me = lax.axis_index("req")
    z = lax.axis_index("tp")
    mx, my, mc = me // 8, (me // 2) % 4, me % 2
    f32, bf16 = jnp.float32, jnp.bfloat16

    def peer(o):
        return ((mx + o[0]) % 4) * 8 + ((my + o[1]) % 4) * 2 + (mc + o[2]) % 2

    own = pl.ds(pl.multiple_of(z * XB, 64), XB)
    loads = [
        pltpu.make_async_copy(x_hbm, xf.at[own], load_sem.at[0]),
        pltpu.make_async_copy(pool_hbm, pool, load_sem.at[1]),
        pltpu.make_async_copy(w_hbm, w, load_sem.at[2]),
        pltpu.make_async_copy(wo_hbm, wo, load_sem.at[3]),
    ]
    for c in loads:
        c.start()
    barrier = pltpu.get_barrier_semaphore()
    for o in OFFSETS:
        pl.semaphore_signal(barrier, inc=1, device_id={"req": peer(o)}, device_id_type=MESH)
    for k in Z_STEPS:
        pl.semaphore_signal(barrier, inc=1, device_id={"tp": lax.rem(z + k, TP)}, device_id_type=MESH)

    pl.semaphore_wait(barrier, len(OFFSETS) + len(Z_STEPS))
    loads[0].wait()

    ags = []
    for k in Z_STEPS:
        copy = pltpu.make_async_remote_copy(
            src_ref=xf.at[own], dst_ref=xf.at[own], send_sem=ag_ss.at[k], recv_sem=ag_rs.at[k],
            device_id={"tp": lax.rem(z + k, TP)}, device_id_type=MESH,
        )
        copy.start()
        ags.append(copy)

    plan = plan_ref[KEEP:, :]
    page_pos = (iota((TAIL, 64), 0) + KEEP) * PAGE
    inside = page_pos < lens_ref[...]
    held = (plan == me) & inside
    held_f = held.astype(f32)
    below = (iota((TAIL, TAIL), 0) > iota((TAIL, TAIL), 1)).astype(f32)
    rank = mm(below, held_f, ((1,), (0,)))
    ones = jnp.ones((8, TAIL), f32)
    count = mm(ones, held_f, ((1,), (0,)))
    r0, r1 = iota((64, 64), 0), iota((64, 64), 1)
    rank = rank + mm(count, ((r1 % 2 == 1) & (r0 == r1 - 1)).astype(f32), ((1,), (0,)))[0:1, :]
    slot_f = table_ref[KEEP:, :].astype(f32)
    pair = (iota((64, 128), 0) // 2 == iota((64, 128), 1)).astype(f32)
    rows = []
    for c in range(2):
        value = jnp.where(held & (rank == c), slot_f, 0.0)
        rows.append(mm(mm(ones, value, ((1,), (0,))), pair, ((1,), (0,)))[0:1, :])

    lane = iota((TAIL, 64), 1)

    def own_column(values):
        cols = [jnp.sum(jnp.where(lane == 2 * me + a, values, 0.0), axis=1, keepdims=True) for a in range(2)]
        return jnp.concatenate(cols, axis=0)

    e0, e1 = iota((2 * TAIL, 128), 0), iota((2 * TAIL, 128), 1)

    def as_row(col):
        return jnp.sum(jnp.where(e0 == e1, col, 0.0), axis=0, keepdims=True)

    group_col, ok_col = own_column(plan.astype(f32)), own_column(inside.astype(f32))
    group_row = as_row(group_col)
    earlier = jnp.where((group_col == group_row) & (e0 < e1), ok_col, 0.0)
    rows.append(as_row(own_column(table_ref[:KEEP, :].astype(f32))))
    rows.append(group_row * 2.0 + as_row(ok_col) * jnp.sum(earlier, axis=0, keepdims=True))
    at_row = iota((8, 128), 0)
    lists = jnp.zeros((8, 128), f32)
    for n, row in enumerate(rows):
        lists = jnp.where(at_row == n, row, lists)
    idx_v[...] = lists.astype(jnp.int32)
    idx_copy = pltpu.make_async_copy(idx_v, idx, load_sem.at[4])
    idx_copy.start()

    loads[1].wait()

    def turn(i, carry):
        for k in range(5):
            lanes = pl.ds(pl.multiple_of(i * WIDTH + k * 128, 128), 128)
            pf[k, pl.ds(pl.multiple_of(i * STEP, 8), POOL), :] = pool[:, lanes].astype(f32)
        return carry

    lax.fori_loop(0, ROWS, turn, 0)
    idx_copy.wait()

    def page_tile(slot, k):
        return pf[k, pl.ds(jnp.clip(slot, 0, POOL - 1), ROWS, stride=STEP), :].astype(bf16)

    def slots(o):
        return 2 if rounds == 2 or o == STATED else 1

    copies = []
    for n, o in enumerate(OFFSETS):
        p = peer(o)
        for c in range(slots(o)):
            slot = idx[c, p]
            for k in range(5):
                send[p, c, :, k * 128 : (k + 1) * 128] = page_tile(slot, k)
        held_slots = pl.ds(0, slots(o))
        copy = pltpu.make_async_remote_copy(
            src_ref=send.at[p, held_slots], dst_ref=recv.at[me, held_slots],
            send_sem=page_ss.at[n], recv_sem=page_rs.at[n], device_id={"req": p}, device_id_type=MESH,
        )
        copy.start()
        copies.append(copy)

    def home_page(e, carry):
        slot = idx[2, e]
        for k in range(5):
            xh[e // KEEP, pl.ds(pl.multiple_of(e % KEEP * ROWS, ROWS), ROWS), k * 128 : (k + 1) * 128] = page_tile(slot, k)
        return carry

    lax.fori_loop(0, 2 * KEEP, home_page, 0)

    lens0, lens1 = lens_s[2 * me], lens_s[2 * me + 1]
    tok = iota((1, 2 * NEW), 1)
    places = jnp.where(tok < NEW, lens0 + tok, lens1 + tok - NEW).astype(f32)
    freq = jnp.exp(iota((HALF, 128), 0).astype(f32) * (-2.0 * LOG_THETA / HD))
    angle = freq * places
    cos_sin[0], cos_sin[1] = jnp.cos(angle), jnp.sin(angle)

    for i in range(20):
        gb[i * 128 : (i + 1) * 128, :] = jnp.transpose(jnp.broadcast_to(gain_ref[i : i + 1, :], (128, 128)))
    loads[3].wait()
    for i in range(20):
        wot[i * 128 : (i + 1) * 128, :] = jnp.transpose(wo[:, i * 128 : (i + 1) * 128])
    group = iota((GROUPS, 64), 0)
    owed = jnp.zeros((GROUPS, 64), f32)
    for j in range(KEEP, KEEP + TAIL):
        owed += ((plan_ref[j : j + 1, :] == group) & (lens_ref[...] > j * PAGE)).astype(f32)
    owed = mm(owed, (iota((64, GROUPS), 0) // 2 == iota((64, GROUPS), 1)).astype(f32), ((1,), (0,)))
    g0, g1 = iota((GROUPS, GROUPS), 0), iota((GROUPS, GROUPS), 1)
    owed = jnp.where(g0 == (g1 + GROUPS // 2) % GROUPS, 0.0, owed)
    more_ref[0] = (jnp.max(owed) > 1.5).astype(jnp.int32)

    loads[2].wait()
    for copy in ags:
        copy.wait_recv()

    xw = xf[...].astype(f32)
    rstd = lax.rsqrt(jnp.sum(xw * xw, axis=0, keepdims=True) * (1.0 / D) + EPSILON)
    normed = (xw * rstd * gb[...]).astype(bf16)
    proj = mm(w[...], normed, ((1,), (0,)))
    cos, sin = cos_sin[0], cos_sin[1]

    def rotated(first):
        front, back = proj[first : first + HALF], proj[first + HALF : first + HD]
        full = jnp.concatenate([front * cos - back * sin, back * cos + front * sin], axis=0)
        return full.astype(bf16)

    def turned(values):
        padded = jnp.concatenate([values.astype(f32), jnp.zeros((128 - HD, 2 * NEW), f32)], axis=0)
        return jnp.transpose(padded).astype(bf16)

    feature, at_lane = iota((HD, QUERY_LANES), 0), iota((HD, QUERY_LANES), 1)
    spread = feature == at_lane
    for _, _, _, stand in KEY_TILE[1:]:
        spread = spread | (feature == at_lane - stand)
    spread = spread.astype(f32).astype(bf16)
    for g in range(G):
        qt = mm(rotated(g * HD), spread, ((0,), (0,))).astype(bf16)
        for a in range(2):
            qs[a, g * NEW : (g + 1) * NEW, :] = qt[a * NEW : (a + 1) * NEW]
    kn[...] = turned(rotated(G * HD))
    vn[...] = turned(proj[(G + 1) * HD :].astype(bf16))

    t_col = iota((G * NEW, 1), 0) % NEW

    def attend(a, keys, first_pos, top0, with_window):
        length = lens_s[2 * me + a]
        cols = iota((1, 512), 1)
        top = top0
        for m, (first, width, at, _) in enumerate(KEY_TILE):
            s = mm(qs[a, :, at : at + width], keys[:, first : first + width], ((1,), (1,)))
            rel = cols * 4 + (first_pos + m) - length
            ok = rel < 0
            if with_window:
                ok = ok & (rel > t_col - WINDOW)
            s = jnp.where(ok, s, MASKED)
            sc[m] = s
            top = jnp.maximum(top, jnp.max(s, axis=1, keepdims=True))
        total = jnp.zeros((G * NEW, 1), f32)
        sums = jnp.zeros((G * NEW, 128), f32)
        for m, (first, width, offset) in enumerate(VAL_TILE):
            p = jnp.exp2((sc[m] - top) * SCALE)
            total = total + jnp.sum(p, axis=1, keepdims=True)
            o = mm(p.astype(bf16), keys[:, first : first + width], ((1,), (0,)))
            sums = sums + pltpu.roll(o, width - offset, 1)[:, :128]
        return top, total, sums

    def home(a, carry):
        at = pl.ds(pl.multiple_of(a * NEW, NEW), NEW)
        s = mm(qs[a, :, :128], kn[at, :], ((1,), (1,)))
        s = jnp.where(iota((G * NEW, NEW), 1) <= t_col, s, MASKED)
        top_new = jnp.max(s, axis=1, keepdims=True)
        top, total, sums = attend(a, xh.at[a], 0, top_new, True)
        p = jnp.exp2((s - top) * SCALE)
        stat[a, 0] = jnp.broadcast_to(top, (G * NEW, 128))
        stat[a, 1] = jnp.broadcast_to(total + jnp.sum(p, axis=1, keepdims=True), (G * NEW, 128))
        acc[a] = sums + mm(p.astype(bf16), vn[at, :], ((1,), (0,)))
        return carry

    lax.fori_loop(0, 2, home, 0)

    for copy in copies:
        copy.wait_recv()

    def tail(a, carry):
        for j in range(TAIL):
            where = jnp.clip(idx[3, a * TAIL + j], 0, 2 * GROUPS - 1)
            xt[j * ROWS : (j + 1) * ROWS, :] = recv[where // 2, where % 2]
        old_top = stat[a, 0][:, :1]
        top, total, sums = attend(a, xt, KEEP * PAGE, old_top, False)
        weight = jnp.exp2((old_top - top) * SCALE)
        result = (acc[a] * weight + sums) / (stat[a, 1][:, :1] * weight + total)
        for g in range(G):
            hs[g, pl.ds(pl.multiple_of(a * NEW, NEW), NEW), :] = result[g * NEW : (g + 1) * NEW]
        return carry

    lax.fori_loop(0, 2, tail, 0)
    for g in range(G):
        ht[g * HD : (g + 1) * HD, :] = jnp.transpose(hs[g])[:HD].astype(bf16)

    def project(dest):
        rows = pl.ds(pl.multiple_of(dest * XB, 64), XB)
        return mm(wot[rows, :], ht[...], ((1,), (0,)))

    for k in Z_STEPS:
        part[k] = project(lax.rem(z + k, TP)).astype(bf16)
    sums = []
    for k in Z_STEPS:
        copy = pltpu.make_async_remote_copy(
            src_ref=part.at[k], dst_ref=rrecv.at[k], send_sem=rs_ss.at[k], recv_sem=rs_rs.at[k],
            device_id={"tp": lax.rem(z + k, TP)}, device_id_type=MESH,
        )
        copy.start()
        sums.append(copy)
    total = project(z)
    for k, copy in reversed(list(zip(Z_STEPS, sums))):
        copy.wait_recv()
        total = total + rrecv[k].astype(f32)
    out_ref[...] = total

    for copy in ags + copies + sums:
        copy.wait_send()


def layer(rounds, *operands):
    any_space = pl.BlockSpec(memory_space=pl.ANY)
    vmem = pl.BlockSpec(memory_space=pltpu.VMEM)
    smem = pl.BlockSpec(memory_space=pltpu.SMEM)
    f32, bf16 = jnp.float32, jnp.bfloat16
    dma = pltpu.SemaphoreType.DMA
    return pl.pallas_call(
        functools.partial(kernel, rounds),
        out_shape=(jax.ShapeDtypeStruct((XB, 128), f32), jax.ShapeDtypeStruct((1,), jnp.int32)),
        in_specs=[any_space, vmem, any_space, any_space, any_space, vmem, vmem, vmem, smem],
        out_specs=(vmem, smem),
        scratch_shapes=[
            pltpu.VMEM((2, HALF, 128), f32),
            pltpu.VMEM((D, 128), bf16),
            pltpu.VMEM((POOL, ROWS * WIDTH), bf16),
            pltpu.VMEM((480, D), bf16),
            pltpu.VMEM((D, 128), f32),
            pltpu.VMEM((XB, D), bf16),
            pltpu.VMEM((D, XB), bf16),
            pltpu.VMEM((5, ROWS * STEP, 128), f32),
            pltpu.VMEM((GROUPS, 2, ROWS, WIDTH), bf16),
            pltpu.VMEM((GROUPS, 2, ROWS, WIDTH), bf16),
            pltpu.VMEM((2, 512, WIDTH), bf16),
            pltpu.VMEM((512, WIDTH), bf16),
            pltpu.VMEM((2, G * NEW, QUERY_LANES), bf16),
            pltpu.VMEM((128, 128), bf16),
            pltpu.VMEM((128, 128), bf16),
            pltpu.VMEM((4, G * NEW, 512), f32),
            pltpu.VMEM((2, 2, G * NEW, 128), f32),
            pltpu.VMEM((2, G * NEW, 128), f32),
            pltpu.VMEM((G, 128, 128), f32),
            pltpu.VMEM((XB, 128), bf16),
            pltpu.VMEM((TP, XB, 128), bf16),
            pltpu.VMEM((TP, XB, 128), bf16),
            pltpu.VMEM((8, 128), jnp.int32),
            pltpu.SMEM((8, 128), jnp.int32),
            dma((5,)), dma((31,)), dma((31,)), dma((TP,)), dma((TP,)), dma((TP,)), dma((TP,)),
        ],
        compiler_params=pltpu.CompilerParams(
            collective_id=rounds, has_side_effects=True, vmem_limit_bytes=60 * 2**20
        ),
        name=f"paged_prefill_{rounds}",
    )(*operands)


def local(activations, norm_gain, input_proj, output_proj, cache_pool, page_table, rebalance_plan, cached_lengths, token_positions):
    operands = (
        activations.T,
        norm_gain.reshape(20, 128),
        jnp.transpose(input_proj, (1, 2, 0)).reshape(480, D),
        output_proj,
        cache_pool.reshape(POOL, ROWS * WIDTH),
        page_table.T,
        rebalance_plan.T,
        cached_lengths.reshape(1, 64),
        cached_lengths,
    )
    out, more = layer(1, *operands)
    out = lax.cond(more[0] > 0, lambda first, *rest: layer(2, *rest)[0], lambda first, *rest: first, out, *operands)
    return out.T


def solution(mesh):
    in_specs = (
        P("req", "tp"), P(), P(None, "tp", None), P("tp", None), P("req", "tp", None), P(), P(), P(), P(),
    )
    return jax.shard_map(local, mesh=mesh, in_specs=in_specs, out_specs=P("req", "tp"), check_vma=False)
```

time: 55.9 us -> 55.6 us (level)
  no operation moved by 1% of the time
where the time goes in v3:
time: 55.6 us; the launch traced here: 55.5 us
  Pallas kernels  53 us (95%)
  local copies, waits for them, and re-layouts  1.61 us (3%)
  between operations  0.61 us (1%)
    pallas_call x1, Pallas kernels, layer(): pl.pallas_call(functools.partial(kernel, rounds), out_shape=(jax.ShapeDty...  53 us
    unnamed x9, local copies, waits for them, and re-layouts  1.61 us

profile of v3, /device:TPU:1, one launch (start us, length us, event | category | flops | bytes accessed | tf_op | source)
XLA Modules:
  0.0 55.5 jit_solution(948148263875998667)
XLA Ops:
  0.0 0.0 copy-start
  0.0 0.0 copy-start.1
  0.0 0.0 copy-start.2
  0.0 0.0 copy-start.3
  0.0 53.0 %paged_prefill_1.1 = (f32[320,128]{1,0:T(8,128)}, s32[1]{0:T(128)}) custom-call(bf16[320,128]{1,0:T(8,128)(2,1)} %bitcast.15, f32[20,128]{1,0:T(8,128)} %bitcast.22, bf16[480,2560]{1,0:T(8,128)(2,1)} %bitcast.13, bf16[320,2560]{1,0:T(8,128)(2,1)} %wo_hbm.1, bf16[94,20480]{1,0:T(8,128)(2,1)} %bitcast.11, s32[32,64]{1,0:T(8,128)} %bitcast.18, ...), custom_call_target="tpu_custom_call" | custom-call | tf_op jit(solution)/shard_map/paged_prefill_1/pallas_call | solution.py:311
  53.6 0.0 copy-done
  53.6 0.0 copy-done.1
  53.6 0.0 copy-done.2
  53.6 0.0 copy-done.3
  53.7 0.2 conditional.1
  53.9 1.6 %copy.12 = f32[128,320]{0,1:T(8,128)} copy(f32[128,320]{0,1:T(8,128)} %bitcast.17) | data formatting | bytes 327680
Async XLA Ops:
  0.0 53.6 %copy-start = (bf16[2560,1,480]{0,2,1:T(8,128)(2,1)S(1)}, bf16[2560,1,480]{0,2,1:T(8,128)(2,1)}, u32[]{:S(2)}) copy-start(bf16[2560,1,480]{0,2,1:T(8,128)(2,1)} %param.13) | copy-start | bytes 7372804
  0.0 53.6 %copy-start.1 = (bf16[320,2560]{1,0:T(8,128)(2,1)S(1)}, bf16[320,2560]{1,0:T(8,128)(2,1)}, u32[]{:S(2)}) copy-start(bf16[320,2560]{1,0:T(8,128)(2,1)} %wo_hbm.1) | copy-start | bytes 4915204
  0.0 53.6 %copy-start.2 = (s32[64,32]{0,1:T(8,128)S(1)}, s32[64,32]{0,1:T(8,128)}, u32[]{:S(2)}) copy-start(s32[64,32]{0,1:T(8,128)} %param.16) | copy-start | bytes 24580
  0.0 53.6 %copy-start.3 = (s32[64,32]{0,1:T(8,128)S(1)}, s32[64,32]{0,1:T(8,128)}, u32[]{:S(2)}) copy-start(s32[64,32]{0,1:T(8,128)} %param.17) | copy-start | bytes 24580

commit v4 on v3

--- a/solution.py
+++ b/solution.py
@@ -27,13 +27,13 @@
 LOG_THETA = 9.210340371976184
 MASKED = -1e30
 SCALE = HD ** (-0.5) * 1.4426950408889634
-STEP = 96
+STEP = 97
 KEY_TILE = ((0, 128, 0, 0), (128, 128, 128, 160), (256, 256, 256, 320), (384, 256, 512, 608))
 QUERY_LANES = 768
 VAL_TILE = ((0, 256, 80), (128, 256, 112), (384, 128, 16), (512, 128, 48))
 OFFSETS = [(x, y, c) for x in range(4) for y in range(4) for c in range(2) if (x, y, c) != (0, 0, 0)]
 OFFSETS.sort(key=lambda o: -min(o[0], 4 - o[0]) - min(o[1], 4 - o[1]))
-Z_STEPS = (4, 3, 5, 2, 6, 1, 7)
+PIECES = 4
 STATED = (2, 0, 0)
 
 
@@ -72,20 +72,33 @@
     barrier = pltpu.get_barrier_semaphore()
     for o in OFFSETS:
         pl.semaphore_signal(barrier, inc=1, device_id={"req": peer(o)}, device_id_type=MESH)
-    for k in Z_STEPS:
-        pl.semaphore_signal(barrier, inc=1, device_id={"tp": lax.rem(z + k, TP)}, device_id_type=MESH)
-
-    pl.semaphore_wait(barrier, len(OFFSETS) + len(Z_STEPS))
+    ring = (lax.rem(z + 1, TP), lax.rem(z + TP - 1, TP))
+    for n in ring:
+        pl.semaphore_signal(barrier, inc=1, device_id={"tp": n}, device_id_type=MESH)
+
+    pl.semaphore_wait(barrier, len(OFFSETS) + len(ring))
     loads[0].wait()
 
-    ags = []
-    for k in Z_STEPS:
-        copy = pltpu.make_async_remote_copy(
-            src_ref=xf.at[own], dst_ref=xf.at[own], send_sem=ag_ss.at[k], recv_sem=ag_rs.at[k],
-            device_id={"tp": lax.rem(z + k, TP)}, device_id_type=MESH,
-        )
-        copy.start()
-        ags.append(copy)
+    ags = {}
+
+    def ag_step(step):
+        for piece in range(PIECES):
+            for way in range(2):
+                if step:
+                    ags[step - 1, way, piece].wait_recv()
+                if step < 4 - way:
+                    block = lax.rem(z - step + TP, TP) if way == 0 else lax.rem(z + step, TP)
+                    size = XB // PIECES
+                    at = pl.ds(pl.multiple_of(block * XB + piece * size, 16), size)
+                    n = (step * 2 + way) * PIECES + piece
+                    copy = pltpu.make_async_remote_copy(
+                        src_ref=xf.at[at], dst_ref=xf.at[at], send_sem=ag_ss.at[n], recv_sem=ag_rs.at[n],
+                        device_id={"tp": ring[way]}, device_id_type=MESH,
+                    )
+                    copy.start()
+                    ags[step, way, piece] = copy
+
+    ag_step(0)
 
     plan = plan_ref[KEEP:, :]
     page_pos = (iota((TAIL, 64), 0) + KEEP) * PAGE
@@ -134,7 +147,7 @@
     def turn(i, carry):
         for k in range(5):
             lanes = pl.ds(pl.multiple_of(i * WIDTH + k * 128, 128), 128)
-            pf[k, pl.ds(pl.multiple_of(i * STEP, 8), POOL), :] = pool[:, lanes].astype(f32)
+            pf[k, pl.ds(i * STEP, POOL), :] = pool[:, lanes].astype(f32)
         return carry
 
     lax.fori_loop(0, ROWS, turn, 0)
@@ -161,6 +174,8 @@
         copy.start()
         copies.append(copy)
 
+    ag_step(1)
+
     def home_page(e, carry):
         slot = idx[2, e]
         for k in range(5):
@@ -168,6 +183,7 @@
         return carry
 
     lax.fori_loop(0, 2 * KEEP, home_page, 0)
+    ag_step(2)
 
     lens0, lens1 = lens_s[2 * me], lens_s[2 * me + 1]
     tok = iota((1, 2 * NEW), 1)
@@ -178,6 +194,7 @@
 
     for i in range(20):
         gb[i * 128 : (i + 1) * 128, :] = jnp.transpose(jnp.broadcast_to(gain_ref[i : i + 1, :], (128, 128)))
+    ag_step(3)
     loads[3].wait()
     for i in range(20):
         wot[i * 128 : (i + 1) * 128, :] = jnp.transpose(wo[:, i * 128 : (i + 1) * 128])
@@ -191,8 +208,8 @@
     more_ref[0] = (jnp.max(owed) > 1.5).astype(jnp.int32)
 
     loads[2].wait()
-    for copy in ags:
-        copy.wait_recv()
+    for piece in range(PIECES):
+        ags[3, 0, piece].wait_recv()
 
     xw = xf[...].astype(f32)
     rstd = lax.rsqrt(jnp.sum(xw * xw, axis=0, keepdims=True) * (1.0 / D) + EPSILON)
@@ -282,23 +299,36 @@
         rows = pl.ds(pl.multiple_of(dest * XB, 64), XB)
         return mm(wot[rows, :], ht[...], ((1,), (0,)))
 
-    for k in Z_STEPS:
-        part[k] = project(lax.rem(z + k, TP)).astype(bf16)
-    sums = []
-    for k in Z_STEPS:
-        copy = pltpu.make_async_remote_copy(
-            src_ref=part.at[k], dst_ref=rrecv.at[k], send_sem=rs_ss.at[k], recv_sem=rs_rs.at[k],
-            device_id={"tp": lax.rem(z + k, TP)}, device_id_type=MESH,
-        )
-        copy.start()
-        sums.append(copy)
-    total = project(z)
-    for k, copy in reversed(list(zip(Z_STEPS, sums))):
-        copy.wait_recv()
-        total = total + rrecv[k].astype(f32)
-    out_ref[...] = total
-
-    for copy in ags + copies + sums:
+    size = XB // PIECES
+    sums = {}
+    for step in range(4):
+        for way in range(2):
+            hop = step - way
+            if hop < 0:
+                continue
+            mine = project(lax.rem(z + 4 - hop, TP) if way == 0 else lax.rem(z + TP - 3 + hop, TP))
+            for piece in range(PIECES):
+                n = (hop * 2 + way) * PIECES + piece
+                block = mine[piece * size : (piece + 1) * size]
+                if hop:
+                    sums[hop - 1, way, piece].wait_recv()
+                    block = block + rrecv[n - 2 * PIECES].astype(f32)
+                part[n] = block.astype(bf16)
+                copy = pltpu.make_async_remote_copy(
+                    src_ref=part.at[n], dst_ref=rrecv.at[n], send_sem=rs_ss.at[n], recv_sem=rs_rs.at[n],
+                    device_id={"tp": ring[way]}, device_id_type=MESH,
+                )
+                copy.start()
+                sums[hop, way, piece] = copy
+    mine = project(z)
+    for piece in range(PIECES):
+        block = mine[piece * size : (piece + 1) * size]
+        for hop, way in ((2, 1), (3, 0)):
+            sums[hop, way, piece].wait_recv()
+            block = block + rrecv[(hop * 2 + way) * PIECES + piece].astype(f32)
+        out_ref[piece * size : (piece + 1) * size, :] = block
+
+    for copy in list(ags.values()) + copies + list(sums.values()):
         copy.wait_send()
 
 
@@ -321,7 +351,7 @@
             pltpu.VMEM((D, 128), f32),
             pltpu.VMEM((XB, D), bf16),
             pltpu.VMEM((D, XB), bf16),
-            pltpu.VMEM((5, ROWS * STEP, 128), f32),
+            pltpu.VMEM((5, ROWS * STEP + 8, 128), f32),
             pltpu.VMEM((GROUPS, 2, ROWS, WIDTH), bf16),
             pltpu.VMEM((GROUPS, 2, ROWS, WIDTH), bf16),
             pltpu.VMEM((2, 512, WIDTH), bf16),
@@ -334,11 +364,11 @@
             pltpu.VMEM((2, G * NEW, 128), f32),
             pltpu.VMEM((G, 128, 128), f32),
             pltpu.VMEM((XB, 128), bf16),
-            pltpu.VMEM((TP, XB, 128), bf16),
-            pltpu.VMEM((TP, XB, 128), bf16),
+            pltpu.VMEM((8 * PIECES, XB // PIECES, 128), bf16),
+            pltpu.VMEM((8 * PIECES, XB // PIECES, 128), bf16),
             pltpu.VMEM((8, 128), jnp.int32),
             pltpu.SMEM((8, 128), jnp.int32),
-            dma((5,)), dma((31,)), dma((31,)), dma((TP,)), dma((TP,)), dma((TP,)), dma((TP,)),
+            dma((5,)), dma((31,)), dma((31,)), *[dma((8 * PIECES,))] * 4,
         ],
         compiler_params=pltpu.CompilerParams(
             collective_id=rounds, has_side_effects=True, vmem_limit_bytes=60 * 2**20

time: 55.6 us -> 52.3 us (0.941)
  the two profiles are of different devices: /device:TPU:1 before, /device:TPU:6 now
where the time goes in v4:
time: 52.3 us; the launch traced here: 52.2 us
  Pallas kernels  49.8 us (95%)
  local copies, waits for them, and re-layouts  1.61 us (3%)
  between operations  0.61 us (1%)
    pallas_call x1, Pallas kernels, layer(): pl.pallas_call(functools.partial(kernel, rounds), out_shape=(jax.ShapeDty...  49.8 us
    unnamed x9, local copies, waits for them, and re-layouts  1.61 us

profile of v4, /device:TPU:6, one launch (start us, length us, event | category | flops | bytes accessed | tf_op | source)
XLA Modules:
  0.0 52.2 jit_solution(4380948990288542281)
XLA Ops:
  0.0 0.0 copy-start
  0.0 0.0 copy-start.1
  0.0 0.0 copy-start.2
  0.0 0.0 copy-start.3
  0.0 49.8 %paged_prefill_1.1 = (f32[320,128]{1,0:T(8,128)}, s32[1]{0:T(128)}) custom-call(bf16[320,128]{1,0:T(8,128)(2,1)} %bitcast.15, f32[20,128]{1,0:T(8,128)} %bitcast.22, bf16[480,2560]{1,0:T(8,128)(2,1)} %bitcast.13, bf16[320,2560]{1,0:T(8,128)(2,1)} %wo_hbm.1, bf16[94,20480]{1,0:T(8,128)(2,1)} %bitcast.11, s32[32,64]{1,0:T(8,128)} %bitcast.18, ...), custom_call_target="tpu_custom_call" | custom-call | tf_op jit(solution)/shard_map/paged_prefill_1/pallas_call | solution.py:341
  50.3 0.0 copy-done
  50.3 0.0 copy-done.1
  50.4 0.0 copy-done.2
  50.4 0.0 copy-done.3
  50.4 0.2 conditional.1
  50.6 1.6 %copy.12 = f32[128,320]{0,1:T(8,128)} copy(f32[128,320]{0,1:T(8,128)} %bitcast.17) | data formatting | bytes 327680
Async XLA Ops:
  0.0 50.3 %copy-start = (bf16[2560,1,480]{0,2,1:T(8,128)(2,1)S(1)}, bf16[2560,1,480]{0,2,1:T(8,128)(2,1)}, u32[]{:S(2)}) copy-start(bf16[2560,1,480]{0,2,1:T(8,128)(2,1)} %param.13) | copy-start | bytes 7372804
  0.0 50.3 %copy-start.1 = (bf16[320,2560]{1,0:T(8,128)(2,1)S(1)}, bf16[320,2560]{1,0:T(8,128)(2,1)}, u32[]{:S(2)}) copy-start(bf16[320,2560]{1,0:T(8,128)(2,1)} %wo_hbm.1) | copy-start | bytes 4915204
  0.0 50.4 %copy-start.2 = (s32[64,32]{0,1:T(8,128)S(1)}, s32[64,32]{0,1:T(8,128)}, u32[]{:S(2)}) copy-start(s32[64,32]{0,1:T(8,128)} %param.16) | copy-start | bytes 24580
  0.0 50.4 %copy-start.3 = (s32[64,32]{0,1:T(8,128)S(1)}, s32[64,32]{0,1:T(8,128)}, u32[]{:S(2)}) copy-start(s32[64,32]{0,1:T(8,128)} %param.17) | copy-start | bytes 24580

commit v5 on v4

--- a/solution.py
+++ b/solution.py
@@ -33,7 +33,7 @@
 VAL_TILE = ((0, 256, 80), (128, 256, 112), (384, 128, 16), (512, 128, 48))
 OFFSETS = [(x, y, c) for x in range(4) for y in range(4) for c in range(2) if (x, y, c) != (0, 0, 0)]
 OFFSETS.sort(key=lambda o: -min(o[0], 4 - o[0]) - min(o[1], 4 - o[1]))
-PIECES = 4
+PIECES = 2
 STATED = (2, 0, 0)
 
 
@@ -47,9 +47,9 @@
 
 def kernel(
     rounds,
-    x_hbm, gain_ref, w_hbm, wo_hbm, pool_hbm, table_ref, plan_ref, lens_ref, lens_s,
+    x_hbm, gain_hbm, w_hbm, wo_hbm, pool_hbm, table_hbm, plan_hbm, lens_hbm,
     out_ref, more_ref,
-    cos_sin, xf, pool, w, gb, wo, wot, pf, send, recv, xh, xt, qs, kn, vn, sc, stat, acc, hs, ht, part, rrecv, idx_v, idx,
+    gain_ref, table_ref, plan_ref, lens_ref, cos_sin, xf, pool, w, gb, wo, wot, pf, send, recv, xh, xt, qs, kn, vn, sc, stat, acc, hs, ht, mine, part, rrecv, idx_v, idx,
     load_sem, page_ss, page_rs, ag_ss, ag_rs, rs_ss, rs_rs,
 ):
     me = lax.axis_index("req")
@@ -66,9 +66,13 @@
         pltpu.make_async_copy(pool_hbm, pool, load_sem.at[1]),
         pltpu.make_async_copy(w_hbm, w, load_sem.at[2]),
         pltpu.make_async_copy(wo_hbm, wo, load_sem.at[3]),
+        pltpu.make_async_copy(table_hbm, table_ref, load_sem.at[5]),
+        pltpu.make_async_copy(plan_hbm, plan_ref, load_sem.at[6]),
+        pltpu.make_async_copy(lens_hbm, lens_ref, load_sem.at[7]),
+        pltpu.make_async_copy(gain_hbm, gain_ref, load_sem.at[8]),
     ]
-    for c in loads:
-        c.start()
+    for n in (0, 4, 5, 6, 1, 7, 2, 3):
+        loads[n].start()
     barrier = pltpu.get_barrier_semaphore()
     for o in OFFSETS:
         pl.semaphore_signal(barrier, inc=1, device_id={"req": peer(o)}, device_id_type=MESH)
@@ -79,6 +83,9 @@
     pl.semaphore_wait(barrier, len(OFFSETS) + len(ring))
     loads[0].wait()
 
+    def crosses(way, piece):
+        return (piece < PIECES // 2) == (way == 0)
+
     ags = {}
 
     def ag_step(step):
@@ -86,7 +93,7 @@
             for way in range(2):
                 if step:
                     ags[step - 1, way, piece].wait_recv()
-                if step < 4 - way:
+                if step < 3 or crosses(way, piece):
                     block = lax.rem(z - step + TP, TP) if way == 0 else lax.rem(z + step, TP)
                     size = XB // PIECES
                     at = pl.ds(pl.multiple_of(block * XB + piece * size, 16), size)
@@ -99,6 +106,9 @@
                     ags[step, way, piece] = copy
 
     ag_step(0)
+
+    for n in (4, 5, 6):
+        loads[n].wait()
 
     plan = plan_ref[KEEP:, :]
     page_pos = (iota((TAIL, 64), 0) + KEEP) * PAGE
@@ -134,6 +144,7 @@
     earlier = jnp.where((group_col == group_row) & (e0 < e1), ok_col, 0.0)
     rows.append(as_row(own_column(table_ref[:KEEP, :].astype(f32))))
     rows.append(group_row * 2.0 + as_row(ok_col) * jnp.sum(earlier, axis=0, keepdims=True))
+    rows.append(jnp.concatenate([lens_ref[...].astype(f32), jnp.zeros((1, 64), f32)], axis=1))
     at_row = iota((8, 128), 0)
     lists = jnp.zeros((8, 128), f32)
     for n, row in enumerate(rows):
@@ -185,12 +196,14 @@
     lax.fori_loop(0, 2 * KEEP, home_page, 0)
     ag_step(2)
 
-    lens0, lens1 = lens_s[2 * me], lens_s[2 * me + 1]
+    lens0, lens1 = idx[4, 2 * me], idx[4, 2 * me + 1]
     tok = iota((1, 2 * NEW), 1)
     places = jnp.where(tok < NEW, lens0 + tok, lens1 + tok - NEW).astype(f32)
     freq = jnp.exp(iota((HALF, 128), 0).astype(f32) * (-2.0 * LOG_THETA / HD))
     angle = freq * places
     cos_sin[0], cos_sin[1] = jnp.cos(angle), jnp.sin(angle)
+
+    loads[7].wait()
 
     for i in range(20):
         gb[i * 128 : (i + 1) * 128, :] = jnp.transpose(jnp.broadcast_to(gain_ref[i : i + 1, :], (128, 128)))
@@ -209,7 +222,7 @@
 
     loads[2].wait()
     for piece in range(PIECES):
-        ags[3, 0, piece].wait_recv()
+        ags[3, int(not crosses(0, piece)), piece].wait_recv()
 
     xw = xf[...].astype(f32)
     rstd = lax.rsqrt(jnp.sum(xw * xw, axis=0, keepdims=True) * (1.0 / D) + EPSILON)
@@ -241,7 +254,7 @@
     t_col = iota((G * NEW, 1), 0) % NEW
 
     def attend(a, keys, first_pos, top0, with_window):
-        length = lens_s[2 * me + a]
+        length = idx[4, 2 * me + a]
         cols = iota((1, 512), 1)
         top = top0
         for m, (first, width, at, _) in enumerate(KEY_TILE):
@@ -295,22 +308,23 @@
     for g in range(G):
         ht[g * HD : (g + 1) * HD, :] = jnp.transpose(hs[g])[:HD].astype(bf16)
 
-    def project(dest):
-        rows = pl.ds(pl.multiple_of(dest * XB, 64), XB)
+    def project(k):
+        rows = pl.ds(pl.multiple_of(lax.rem(z + k, TP) * XB, 64), XB)
         return mm(wot[rows, :], ht[...], ((1,), (0,)))
 
     size = XB // PIECES
     sums = {}
-    for step in range(4):
-        for way in range(2):
-            hop = step - way
-            if hop < 0:
-                continue
-            mine = project(lax.rem(z + 4 - hop, TP) if way == 0 else lax.rem(z + TP - 3 + hop, TP))
-            for piece in range(PIECES):
+    for hop in range(4):
+        if hop < 2:
+            for k in ((4,), (3, 5, 2, 6, 1, 7, 0))[hop]:
+                mine[k] = project(k)
+        for piece in range(PIECES):
+            for way in range(2):
+                if hop == 0 and not crosses(way, piece):
+                    continue
                 n = (hop * 2 + way) * PIECES + piece
-                block = mine[piece * size : (piece + 1) * size]
-                if hop:
+                block = mine[4 - hop if way == 0 else 4 + hop, piece * size : (piece + 1) * size, :]
+                if (hop - 1, way, piece) in sums:
                     sums[hop - 1, way, piece].wait_recv()
                     block = block + rrecv[n - 2 * PIECES].astype(f32)
                 part[n] = block.astype(bf16)
@@ -320,12 +334,11 @@
                 )
                 copy.start()
                 sums[hop, way, piece] = copy
-    mine = project(z)
     for piece in range(PIECES):
-        block = mine[piece * size : (piece + 1) * size]
-        for hop, way in ((2, 1), (3, 0)):
-            sums[hop, way, piece].wait_recv()
-            block = block + rrecv[(hop * 2 + way) * PIECES + piece].astype(f32)
+        block = mine[0, piece * size : (piece + 1) * size, :]
+        for way in range(2):
+            sums[3, way, piece].wait_recv()
+            block = block + rrecv[(6 + way) * PIECES + piece].astype(f32)
         out_ref[piece * size : (piece + 1) * size, :] = block
 
     for copy in list(ags.values()) + copies + list(sums.values()):
@@ -340,10 +353,14 @@
     dma = pltpu.SemaphoreType.DMA
     return pl.pallas_call(
         functools.partial(kernel, rounds),
-        out_shape=(jax.ShapeDtypeStruct((XB, 128), f32), jax.ShapeDtypeStruct((1,), jnp.int32)),
-        in_specs=[any_space, vmem, any_space, any_space, any_space, vmem, vmem, vmem, smem],
+        out_shape=(pltpu.VMEM((XB, 128), f32), jax.ShapeDtypeStruct((1,), jnp.int32)),
+        in_specs=[any_space] * 8,
         out_specs=(vmem, smem),
         scratch_shapes=[
+            pltpu.VMEM((20, 128), f32),
+            pltpu.VMEM((32, 64), jnp.int32),
+            pltpu.VMEM((32, 64), jnp.int32),
+            pltpu.VMEM((1, 64), jnp.int32),
             pltpu.VMEM((2, HALF, 128), f32),
             pltpu.VMEM((D, 128), bf16),
             pltpu.VMEM((POOL, ROWS * WIDTH), bf16),
@@ -364,11 +381,12 @@
             pltpu.VMEM((2, G * NEW, 128), f32),
             pltpu.VMEM((G, 128, 128), f32),
             pltpu.VMEM((XB, 128), bf16),
+            pltpu.VMEM((TP, XB, 128), f32),
             pltpu.VMEM((8 * PIECES, XB // PIECES, 128), bf16),
             pltpu.VMEM((8 * PIECES, XB // PIECES, 128), bf16),
             pltpu.VMEM((8, 128), jnp.int32),
             pltpu.SMEM((8, 128), jnp.int32),
-            dma((5,)), dma((31,)), dma((31,)), *[dma((8 * PIECES,))] * 4,
+            dma((9,)), dma((31,)), dma((31,)), *[dma((8 * PIECES,))] * 4,
         ],
         compiler_params=pltpu.CompilerParams(
             collective_id=rounds, has_side_effects=True, vmem_limit_bytes=60 * 2**20
@@ -387,7 +405,6 @@
         page_table.T,
         rebalance_plan.T,
         cached_lengths.reshape(1, 64),
-        cached_lengths,
     )
     out, more = layer(1, *operands)
     out = lax.cond(more[0] > 0, lambda first, *rest: layer(2, *rest)[0], lambda first, *rest: first, out, *operands)

time: 52.3 us -> 49.7 us (0.950)
  Pallas kernels: 49.8 us -> 48 us
  local copies, waits for them, and re-layouts: 1.61 us -> 0.69 us
    pallas_call x1, Pallas kernels: 49.8 us -> 48 us  [layer(): pl.pallas_call(functools.partial(kernel, rounds), out_shape=(pltpu.VMEM((...]
    unnamed x9 -> x13, local copies, waits for them, and re-layouts: 1.61 us -> 0.69 us
where the time goes in v5:
time: 49.7 us; the launch traced here: 49.6 us
  Pallas kernels  48 us (97%)
  between operations  0.72 us (1%)
  local copies, waits for them, and re-layouts  0.69 us (1%)
    pallas_call x1, Pallas kernels, layer(): pl.pallas_call(functools.partial(kernel, rounds), out_shape=(pltpu.VMEM((...  48 us

profile of v5, /device:TPU:6, one launch (start us, length us, event | category | flops | bytes accessed | tf_op | source)
XLA Modules:
  0.0 49.6 jit_solution(11457814164578859416)
XLA Ops:
  0.0 0.0 copy-start
  0.0 0.0 copy-start.1
  0.0 0.0 copy-start.2
  0.0 0.0 copy-start.3
  0.0 0.0 copy-start.4
  0.0 0.0 copy-start.5
  0.0 48.0 %paged_prefill_1.1 = (f32[320,128]{1,0:T(8,128)S(1)}, s32[1]{0:T(128)}) custom-call(bf16[320,128]{1,0:T(8,128)(2,1)} %bitcast.16, f32[20,128]{1,0:T(8,128)} %bitcast.22, bf16[480,2560]{1,0:T(8,128)(2,1)} %bitcast.14, bf16[320,2560]{1,0:T(8,128)(2,1)} %wo_hbm.1, bf16[94,20480]{1,0:T(8,128)(2,1)} %bitcast.12, s32[32,64]{1,0:T(8,128)} %bitcast.18, ...), custom_call_target="tpu_custom_call" | custom-call | tf_op jit(solution)/shard_map/paged_prefill_1/pallas_call | solution.py:354
  48.7 0.0 copy-done
  48.7 0.0 copy-done.1
  48.7 0.0 copy-done.2
  48.7 0.0 copy-done.3
  48.7 0.0 copy-done.4
  48.7 0.0 copy-done.5
  48.7 0.2 conditional.1
  48.9 0.7 %copy.12 = f32[128,320]{0,1:T(8,128)} copy(f32[128,320]{0,1:T(8,128)S(1)} %bitcast.11) | data formatting | bytes 327680
Async XLA Ops:
  0.0 48.7 %copy-start = (bf16[2560,1,480]{0,2,1:T(8,128)(2,1)S(1)}, bf16[2560,1,480]{0,2,1:T(8,128)(2,1)}, u32[]{:S(2)}) copy-start(bf16[2560,1,480]{0,2,1:T(8,128)(2,1)} %param.13) | copy-start | bytes 7372804
  0.0 48.7 %copy-start.1 = (bf16[128,320]{0,1:T(8,128)(2,1)S(1)}, bf16[128,320]{0,1:T(8,128)(2,1)}, u32[]{:S(2)}) copy-start(bf16[128,320]{0,1:T(8,128)(2,1)} %param.11) | copy-start | bytes 245764
  0.0 48.7 %copy-start.2 = (s32[64,32]{0,1:T(8,128)S(1)}, s32[64,32]{0,1:T(8,128)}, u32[]{:S(2)}) copy-start(s32[64,32]{0,1:T(8,128)} %param.16) | copy-start | bytes 24580
  0.0 48.7 %copy-start.3 = (s32[64,32]{0,1:T(8,128)S(1)}, s32[64,32]{0,1:T(8,128)}, u32[]{:S(2)}) copy-start(s32[64,32]{0,1:T(8,128)} %param.17) | copy-start | bytes 24580
  0.0 48.7 %copy-start.4 = (f32[2560]{0:T(1024)S(1)}, f32[2560]{0:T(1024)}, u32[]{:S(2)}) copy-start(f32[2560]{0:T(1024)} %param.12) | copy-start | bytes 30724
  0.0 48.7 %copy-start.5 = (s32[64]{0:T(128)S(1)}, s32[64]{0:T(128)}, u32[]{:S(2)}) copy-start(s32[64]{0:T(128)} %param.18) | copy-start | bytes 772

commit v6 on v5

--- a/solution.py
+++ b/solution.py
@@ -61,17 +61,19 @@
         return ((mx + o[0]) % 4) * 8 + ((my + o[1]) % 4) * 2 + (mc + o[2]) % 2
 
     own = pl.ds(pl.multiple_of(z * XB, 64), XB)
+    halves = [pl.ds(h * ROWS // 2 * WIDTH, ROWS // 2 * WIDTH) for h in range(2)]
     loads = [
         pltpu.make_async_copy(x_hbm, xf.at[own], load_sem.at[0]),
-        pltpu.make_async_copy(pool_hbm, pool, load_sem.at[1]),
+        pltpu.make_async_copy(pool_hbm.at[:, halves[0]], pool.at[:, halves[0]], load_sem.at[1]),
         pltpu.make_async_copy(w_hbm, w, load_sem.at[2]),
         pltpu.make_async_copy(wo_hbm, wo, load_sem.at[3]),
         pltpu.make_async_copy(table_hbm, table_ref, load_sem.at[5]),
         pltpu.make_async_copy(plan_hbm, plan_ref, load_sem.at[6]),
         pltpu.make_async_copy(lens_hbm, lens_ref, load_sem.at[7]),
         pltpu.make_async_copy(gain_hbm, gain_ref, load_sem.at[8]),
+        pltpu.make_async_copy(pool_hbm.at[:, halves[1]], pool.at[:, halves[1]], load_sem.at[9]),
     ]
-    for n in (0, 4, 5, 6, 1, 7, 2, 3):
+    for n in (0, 4, 5, 6, 1, 8, 7, 2, 3):
         loads[n].start()
     barrier = pltpu.get_barrier_semaphore()
     for o in OFFSETS:
@@ -153,17 +155,12 @@
     idx_copy = pltpu.make_async_copy(idx_v, idx, load_sem.at[4])
     idx_copy.start()
 
-    loads[1].wait()
-
     def turn(i, carry):
         for k in range(5):
             lanes = pl.ds(pl.multiple_of(i * WIDTH + k * 128, 128), 128)
             pf[k, pl.ds(i * STEP, POOL), :] = pool[:, lanes].astype(f32)
         return carry
 
-    lax.fori_loop(0, ROWS, turn, 0)
-    idx_copy.wait()
-
     def page_tile(slot, k):
         return pf[k, pl.ds(jnp.clip(slot, 0, POOL - 1), ROWS, stride=STEP), :].astype(bf16)
 
@@ -171,20 +168,26 @@
         return 2 if rounds == 2 or o == STATED else 1
 
     copies = []
-    for n, o in enumerate(OFFSETS):
-        p = peer(o)
-        for c in range(slots(o)):
-            slot = idx[c, p]
-            for k in range(5):
-                send[p, c, :, k * 128 : (k + 1) * 128] = page_tile(slot, k)
-        held_slots = pl.ds(0, slots(o))
-        copy = pltpu.make_async_remote_copy(
-            src_ref=send.at[p, held_slots], dst_ref=recv.at[me, held_slots],
-            send_sem=page_ss.at[n], recv_sem=page_rs.at[n], device_id={"req": p}, device_id_type=MESH,
-        )
-        copy.start()
-        copies.append(copy)
-
+    for half, load in enumerate((loads[1], loads[8])):
+        load.wait()
+        first, count = half * ROWS // 2, ROWS // 2
+        lax.fori_loop(first, first + count, turn, 0)
+        if half == 0:
+            idx_copy.wait()
+        at = pl.ds(first, count)
+        for n, o in enumerate(OFFSETS):
+            p = peer(o)
+            for c in range(slots(o)):
+                row = jnp.clip(idx[c, p], 0, POOL - 1) + first * STEP
+                for k in range(5):
+                    send[p, c, at, k * 128 : (k + 1) * 128] = pf[k, pl.ds(row, count, stride=STEP), :].astype(bf16)
+            held_slots = pl.ds(0, slots(o))
+            copy = pltpu.make_async_remote_copy(
+                src_ref=send.at[p, held_slots, at], dst_ref=recv.at[me, held_slots, at],
+                send_sem=page_ss.at[half, n], recv_sem=page_rs.at[half, n], device_id={"req": p}, device_id_type=MESH,
+            )
+            copy.start()
+            copies.append(copy)
     ag_step(1)
 
     def home_page(e, carry):
@@ -386,7 +389,7 @@
             pltpu.VMEM((8 * PIECES, XB // PIECES, 128), bf16),
             pltpu.VMEM((8, 128), jnp.int32),
             pltpu.SMEM((8, 128), jnp.int32),
-            dma((9,)), dma((31,)), dma((31,)), *[dma((8 * PIECES,))] * 4,
+            dma((10,)), dma((2, 31)), dma((2, 31)), *[dma((8 * PIECES,))] * 4,
         ],
         compiler_params=pltpu.CompilerParams(
             collective_id=rounds, has_side_effects=True, vmem_limit_bytes=60 * 2**20

time: 49.7 us -> 49.6 us (level); the launches traced: 49.6 us -> 48.8 us
  Pallas kernels: 48 us -> 47.2 us
    pallas_call x1, Pallas kernels: 48 us -> 47.2 us  [layer(): pl.pallas_call(functools.partial(kernel, rounds), out_shape=(pltpu.VMEM((...]
where the time goes in v6:
time: 49.6 us; the launch traced here: 48.8 us
  Pallas kernels  47.2 us (95%)
  between operations  0.72 us (1%)
  local copies, waits for them, and re-layouts  0.69 us (1%)
    pallas_call x1, Pallas kernels, layer(): pl.pallas_call(functools.partial(kernel, rounds), out_shape=(pltpu.VMEM((...  47.2 us

profile of v6, /device:TPU:6, one launch (start us, length us, event | category | flops | bytes accessed | tf_op | source)
XLA Modules:
  0.0 48.8 jit_solution(11375718574238043271)
XLA Ops:
  0.0 0.0 copy-start
  0.0 0.0 copy-start.1
  0.0 0.0 copy-start.2
  0.0 0.0 copy-start.3
  0.0 0.0 copy-start.4
  0.0 0.0 copy-start.5
  0.0 47.2 %paged_prefill_1.1 = (f32[320,128]{1,0:T(8,128)S(1)}, s32[1]{0:T(128)}) custom-call(bf16[320,128]{1,0:T(8,128)(2,1)} %bitcast.16, f32[20,128]{1,0:T(8,128)} %bitcast.22, bf16[480,2560]{1,0:T(8,128)(2,1)} %bitcast.14, bf16[320,2560]{1,0:T(8,128)(2,1)} %wo_hbm.1, bf16[94,20480]{1,0:T(8,128)(2,1)} %bitcast.12, s32[32,64]{1,0:T(8,128)} %bitcast.18, ...), custom_call_target="tpu_custom_call" | custom-call | tf_op jit(solution)/shard_map/paged_prefill_1/pallas_call | solution.py:357
  47.9 0.0 copy-done
  47.9 0.0 copy-done.1
  47.9 0.0 copy-done.2
  47.9 0.0 copy-done.3
  47.9 0.0 copy-done.4
  48.0 0.0 copy-done.5
  48.0 0.2 conditional.1
  48.2 0.7 %copy.12 = f32[128,320]{0,1:T(8,128)} copy(f32[128,320]{0,1:T(8,128)S(1)} %bitcast.11) | data formatting | bytes 327680
Async XLA Ops:
  0.0 47.9 %copy-start = (bf16[2560,1,480]{0,2,1:T(8,128)(2,1)S(1)}, bf16[2560,1,480]{0,2,1:T(8,128)(2,1)}, u32[]{:S(2)}) copy-start(bf16[2560,1,480]{0,2,1:T(8,128)(2,1)} %param.13) | copy-start | bytes 7372804
  0.0 47.9 %copy-start.1 = (bf16[128,320]{0,1:T(8,128)(2,1)S(1)}, bf16[128,320]{0,1:T(8,128)(2,1)}, u32[]{:S(2)}) copy-start(bf16[128,320]{0,1:T(8,128)(2,1)} %param.11) | copy-start | bytes 245764
  0.0 47.9 %copy-start.2 = (s32[64,32]{0,1:T(8,128)S(1)}, s32[64,32]{0,1:T(8,128)}, u32[]{:S(2)}) copy-start(s32[64,32]{0,1:T(8,128)} %param.16) | copy-start | bytes 24580
  0.0 47.9 %copy-start.3 = (s32[64,32]{0,1:T(8,128)S(1)}, s32[64,32]{0,1:T(8,128)}, u32[]{:S(2)}) copy-start(s32[64,32]{0,1:T(8,128)} %param.17) | copy-start | bytes 24580
  0.0 47.9 %copy-start.4 = (f32[2560]{0:T(1024)S(1)}, f32[2560]{0:T(1024)}, u32[]{:S(2)}) copy-start(f32[2560]{0:T(1024)} %param.12) | copy-start | bytes 30724
  0.0 47.9 %copy-start.5 = (s32[64]{0:T(128)S(1)}, s32[64]{0:T(128)}, u32[]{:S(2)}) copy-start(s32[64]{0:T(128)} %param.18) | copy-start | bytes 772
